TPU v7x, 128 devices: a whole 4x4x4 slice. The times are simulated.
128 devices in a mesh: traj: 4 (over y_lo, core), tx: 8 (over y_hi, z), ty: 4 (over x).
Axes of the slice: x: 4, y: 4 (y_hi: 2, y_lo: 2; y = y_hi * 2 + y_lo), z: 4, core: 2. Of those that a mesh axis runs over, the one named last changes fastest.
Arguments:
- density: float32 [4, 256, 4096], P('traj', None, ('tx', 'ty')), may hold values from 1 to 2
- momentum: float32 [4, 2, 256, 4096], P('traj', None, None, ('tx', 'ty')), may hold values from -0.5 to 0.5
- tracer: float32 [4, 256, 4096], P('traj', None, ('tx', 'ty')), may hold values from -1 to 1
- cotangent: float32 [4, 4, 256, 4096], P('traj', None, None, ('tx', 'ty')), may hold values from -6 to 6
- w_in: float32 [32, 16], replicated, may hold values from -1.5 to 1.5
- b_in: float32 [32], replicated, may hold values from -3 to 3
- w_mid: float32 [32, 32], replicated, may hold values from -1 to 1
- b_mid: float32 [32], replicated, may hold values from -3 to 3
- w_out: float32 [8, 32], replicated, may hold values from -1 to 1
- b_out: float32 [8], replicated, may hold values from -3 to 3
Outputs:
- grad_density: float32 [4, 256, 4096], P('traj', None, ('tx', 'ty'))
- grad_momentum: float32 [4, 2, 256, 4096], P('traj', None, None, ('tx', 'ty'))
- grad_tracer: float32 [4, 256, 4096], P('traj', None, ('tx', 'ty'))
- grad_w_in: float32 [32, 16], replicated
- grad_b_in: float32 [32], replicated
- grad_w_mid: float32 [32, 32], replicated
- grad_b_mid: float32 [32], replicated
- grad_w_out: float32 [8, 32], replicated
- grad_b_out: float32 [8], replicated
All inputs are finite; a program needn't handle non-finite values.
Results may differ from a plain program's by a relative error of at most 0.0003.
Values sent between devices are 32-bit elements; how exact they have to be, the bound alone decides.
A program may use at most 128 MiB of HBM per device.

v0:
```python
import jax
import jax.numpy as jnp
from jax import lax
from jax.experimental import pallas as pl
from jax.experimental.pallas import tpu as pltpu
from jax.sharding import PartitionSpec as P

F32 = jnp.float32
BF16 = jnp.bfloat16
courant = 0.1
slope_gain = 0.25
HALO = 4
RING = ("tx", "ty")
Y_ORDER = (0, 2, 1, 3)


def split(x):
    hi = x.astype(BF16)
    return hi, (x - hi.astype(F32)).astype(BF16)


def split3(x):
    hi = x.astype(BF16)
    rest = x - hi.astype(F32)
    mid = rest.astype(BF16)
    return hi, mid, (rest - mid.astype(F32)).astype(BF16)


def six(parts, ones):
    hi, mid, low = parts
    return rows(hi, mid, low, hi, mid, hi, ones)


def dot(a, b):
    return lax.dot_general(a, b, (((1,), (0,)), ((), ())), preferred_element_type=F32)


def dot_nt(a, b):
    return lax.dot_general(a, b, (((1,), (1,)), ((), ())), preferred_element_type=F32)


def exact(a, b, nt=False):
    dims = (((1,), (1 if nt else 0,)), ((), ()))
    return lax.dot_general(a, b, dims, preferred_element_type=F32, precision=lax.Precision.HIGHEST)


def rows(*parts):
    return jnp.concatenate(parts, 0)


def lanes(*parts):
    return jnp.concatenate(parts, 1)


def roll(v, amount):
    return pltpu.roll(v, amount % v.shape[1], 1)


def halves_at(lead, at):
    return [tuple(lead) + (t, at, slice(None)) for t in range(2)]


def get(ref, lead, at):
    return lanes(*[ref[where] for where in halves_at(lead, at)])


def put(ref, lead, at, value):
    for t, where in enumerate(halves_at(lead, at)):
        ref[where] = value[:, 128 * t : 128 * t + 128]


def face_states(cells, gates):
    below, here, above, above2 = cells
    slope_left = [above[c] - below[c] for c in range(4)]
    slope_right = [above2[c] - here[c] for c in range(4)]
    left = [here[c] + slope_gain * gates[c] * slope_left[c] for c in range(4)]
    right = [above[c] - slope_gain * gates[4 + c] * slope_right[c] for c in range(4)]
    return slope_left, slope_right, left, right


def flux_of(left, right):
    u_left = left[1] * (1.0 / left[0])
    u_right = right[1] * (1.0 / right[0])
    speed = 0.5 * jnp.maximum(jnp.abs(u_left), jnp.abs(u_right)) + 0.5
    physical = (
        left[1] + right[1],
        left[1] * u_left + left[0] + (right[1] * u_right + right[0]),
        left[2] * u_left + right[2] * u_right,
        left[3] * u_left + right[3] * u_right,
    )
    return [0.5 * physical[c] - speed * (right[c] - left[c]) for c in range(4)]


def flux_back(cells, gates, cot):
    slope_left, slope_right, left, right = face_states(cells, gates)
    inv_left = 1.0 / left[0]
    inv_right = 1.0 / right[0]
    u_left = left[1] * inv_left
    u_right = right[1] * inv_right
    abs_left = jnp.abs(u_left)
    abs_right = jnp.abs(u_right)
    half = [0.5 * v for v in cot]
    speed = jnp.maximum(abs_left, abs_right) + 1.0
    d_speed = half[0] * (left[0] - right[0])
    for c in range(1, 4):
        d_speed = d_speed + half[c] * (left[c] - right[c])
    share_left = jnp.where(abs_left > abs_right, 1.0, jnp.where(abs_left < abs_right, 0.0, 0.5))
    d_abs_left = d_speed * share_left
    d_abs_right = d_speed - d_abs_left

    def one_side(state, inv, u, d_abs, sign):
        signed = jnp.where(u > 0.0, d_abs, jnp.where(u < 0.0, -d_abs, 0.0))
        d_u = half[1] * state[1] + half[2] * state[2] + half[3] * state[3] + signed
        d_u = d_u * inv
        visc = [sign * (speed * half[c]) for c in range(4)]
        return (
            half[1] - d_u * u + visc[0],
            half[0] + half[1] * u + d_u + visc[1],
            half[2] * u + visc[2],
            half[3] * u + visc[3],
        )

    d_left = one_side(left, inv_left, u_left, d_abs_left, 1.0)
    d_right = one_side(right, inv_right, u_right, d_abs_right, -1.0)
    scaled_left = [slope_gain * v for v in d_left]
    scaled_right = [slope_gain * v for v in d_right]
    d_gates = [scaled_left[c] * slope_left[c] for c in range(4)]
    d_gates += [-(scaled_right[c] * slope_right[c]) for c in range(4)]
    minus_below = [gates[c] * scaled_left[c] for c in range(4)]
    minus_above2 = [gates[4 + c] * scaled_right[c] for c in range(4)]
    to_here = [d_left[c] + minus_above2[c] for c in range(4)]
    to_above = [d_right[c] + minus_below[c] for c in range(4)]
    return d_gates, minus_below, to_here, to_above, minus_above2


def kernel(
    density, momentum, tracer, cotangent, halo,
    w_x, w_y, w_m, w_o, w_ot, w_mt, w_xt, w_yt,
    g_density, g_momentum, g_tracer, packed,
    nat, cot, mid, mid_hi, mid_lo, mid_lo2,
    h1_hi, h1_lo, h2_hi, h2_lo, t_hi, t_lo, gate_x,
    face, d_mix, out_nat,
    xi, gi, di, mi, zi,
    acc_x, acc_y, acc_m, acc_o,
):
    width = nat.shape[2]
    own = density.shape[2]
    blocks = own // 8
    ones = jnp.ones((16, width), BF16)

    for c in range(4):
        if c == 0:
            source = density[0]
        elif c == 3:
            source = tracer[0]
        else:
            source = momentum[0, c - 1]
        nat[c, 8 : 8 + own, :] = source.T
        nat[c, 0:8, :] = halo[c]
        put(cot, (c,), pl.ds(8, own), cotangent[0, c].T)
        put(cot, (c,), pl.ds(0, 8), halo[4 + c])
        put(cot, (c,), pl.ds(8 + own, 8), halo[4 + c])
    acc_x[...] = jnp.zeros_like(acc_x)
    acc_y[...] = jnp.zeros_like(acc_y)
    acc_m[...] = jnp.zeros_like(acc_m)
    acc_o[...] = jnp.zeros_like(acc_o)

    def upper_layers(first):
        first_parts = split3(first)
        seconds, gate_rows = [], []
        for line in range(4):
            at = slice(32 * line, 32 * line + 32)
            operand = six([part[at] for part in first_parts], ones)
            second = split3(jnp.tanh(dot(w_m[...], operand)))
            seconds.append(second)
            gate_rows.append(jnp.tanh(dot(w_o[...], six(second, ones))))
        return (
            first_parts[0],
            first_parts[1],
            rows(*[v[0] for v in seconds]),
            rows(*[v[1] for v in seconds]),
            rows(*gate_rows),
        )

    def limiter_back(gates, d_gates, load_first, load_second):
        for g in range(8):
            put(di, (), pl.ds(g, 8, stride=8), d_gates[g] * (1.0 - gates[g] * gates[g]))
        d_first, mid_lhs, mid_rhs, out_lhs, out_rhs = [], [], [], [], []
        for pair in range(4):
            o_hi, o_lo = split(get(di, (), pl.ds(16 * pair, 16)))
            s_hi, s_lo = load_second(pair)
            f_hi, f_lo = load_first(pair)
            second = s_hi.astype(F32) + s_lo.astype(F32)
            d_second = dot(w_ot[...], rows(o_hi, o_lo, o_hi)) * (1.0 - second * second)
            m_hi, m_lo = split(d_second)
            first = f_hi.astype(F32) + f_lo.astype(F32)
            d_one = dot(w_mt[...], rows(m_hi, m_lo, m_hi)) * (1.0 - first * first)
            d_first.append(split(d_one))
            for line in range(2):
                at = slice(32 * line, 32 * line + 32)
                mid_lhs.append(rows(m_hi[at], m_lo[at]))
                mid_rhs.append(rows(f_hi[at], f_lo[at], ones))
            out_lhs.append(rows(o_hi, o_lo))
            out_rhs.append(rows(s_hi, s_lo, ones))
        acc_m[...] += dot_nt(lanes(*mid_lhs), lanes(*mid_rhs))
        acc_o[...] += dot_nt(lanes(*out_lhs), lanes(*out_rhs))
        return d_first

    def x_forward(b, carry):
        n0 = pl.multiple_of(8 * b, 8)
        here = [nat[c, pl.ds(n0, 8), :] for c in range(4)]
        cells = [[roll(v, 1) for v in here], here, [roll(v, -1) for v in here], [roll(v, -2) for v in here]]
        for s in range(4):
            for c in range(4):
                put(xi, (), pl.ds(4 * s + c, 8, stride=16), cells[s][c])
        for q in range(2):
            window = split3(get(xi, (), pl.ds(64 * q, 64)))
            at = pl.ds(pl.multiple_of(128 * b + 64 * q, 64), 64)
            t_hi[at, :] = window[0]
            t_lo[at, :] = window[1]
            firsts = []
            for line in range(4):
                at = slice(16 * line, 16 * line + 16)
                firsts.append(dot(w_x[...], six([part[at] for part in window], ones)))
            first = jnp.tanh(rows(*firsts))
            f_hi, f_lo, s_hi, s_lo, gate_rows = upper_layers(first)
            at = pl.ds(pl.multiple_of(256 * b + 128 * q, 128), 128)
            h1_hi[at, :] = f_hi
            h1_lo[at, :] = f_lo
            h2_hi[at, :] = s_hi
            h2_lo[at, :] = s_lo
            put(gi, (), pl.ds(32 * q, 32), gate_rows)
        gates = [get(gi, (), pl.ds(g, 8, stride=8)) for g in range(8)]
        for g in range(8):
            gate_x[g, pl.ds(n0, 8), :] = gates[g]
        _, _, left, right = face_states(cells, gates)
        fluxes = flux_of(left, right)
        for c in range(4):
            value = here[c] - courant * (fluxes[c] - roll(fluxes[c], 1))
            put(mid, (c,), pl.ds(n0, 8), value)
            put(mi, (), pl.ds(Y_ORDER[c], 8, stride=4), value)
        at = pl.ds(pl.multiple_of(32 * b, 32), 32)
        for ref, part in zip((mid_hi, mid_lo, mid_lo2), split3(get(mi, (), pl.ds(0, 32)))):
            ref[at, :] = part
        return carry

    lax.fori_loop(0, blocks + 1, x_forward, 0)
    mid[:, :, 8 + own : 16 + own, :] = mid[:, :, 0:8, :]
    for ref in (mid_hi, mid_lo, mid_lo2):
        ref[4 * own + 32 : 4 * own + 64, :] = ref[0:32, :]
    d_mix[:, 0:16, :] = jnp.zeros((2, 16, 128), F32)

    def y_sweep(b, carry):
        n0 = pl.multiple_of(8 * b, 8)
        saved, windows = [], []
        for q in range(2):
            at = pl.ds(pl.multiple_of(32 * b + 16 * q, 16), 32)
            window = mid_hi[at, :], mid_lo[at, :], mid_lo2[at, :]
            windows.append(rows(window[0], window[1], ones))
            first = jnp.tanh(dot(w_y[...], six(window, ones)))
            parts = upper_layers(first)
            saved.append(parts)
            put(gi, (), pl.ds(32 * q, 32), parts[4])
        gates = [get(gi, (), pl.ds(g, 8, stride=8)) for g in range(8)]
        cells = [[get(mid, (c,), pl.ds(n0 + k, 8)) for c in Y_ORDER] for k in range(4)]
        cots = [courant * (get(cot, (c,), pl.ds(n0 + 2, 8)) - get(cot, (c,), pl.ds(n0 + 1, 8))) for c in Y_ORDER]
        d_gates, minus_below, to_here, to_above, minus_above2 = flux_back(cells, gates, cots)
        for c in range(4):
            to = Y_ORDER[c]
            put(face, (to,), pl.ds(n0, 8), minus_below[c])
            put(face, (4 + to,), pl.ds(n0, 8), to_here[c])
            put(face, (8 + to,), pl.ds(n0, 8), to_above[c])
            put(face, (12 + to,), pl.ds(n0, 8), minus_above2[c])

        def load(part):
            def of(pair):
                at = slice(64 * (pair % 2), 64 * (pair % 2) + 64)
                return saved[pair // 2][part][at], saved[pair // 2][part + 1][at]
            return of

        d_first = limiter_back(gates, d_gates, load(0), load(2))
        outs, right_side = [], []
        for q in range(2):
            hi = rows(d_first[2 * q][0], d_first[2 * q + 1][0])
            lo = rows(d_first[2 * q][1], d_first[2 * q + 1][1])
            outs.append(dot(w_yt[...], rows(hi, lo, hi)))
            right_side.append(rows(hi, lo))
        at = pl.multiple_of(32 * b, 32)
        put(d_mix, (), pl.ds(at, 16), get(d_mix, (), pl.ds(at, 16)) + outs[0][:16])
        put(d_mix, (), pl.ds(at + 16, 16), outs[0][16:] + outs[1][:16])
        put(d_mix, (), pl.ds(at + 32, 16), outs[1][16:])
        acc_y[...] += dot_nt(lanes(*windows), lanes(*right_side))

        @pl.when(b == 0)
        def _():
            acc_y[...] = jnp.zeros_like(acc_y)
            acc_m[...] = jnp.zeros_like(acc_m)
            acc_o[...] = jnp.zeros_like(acc_o)

        return carry

    lax.fori_loop(0, blocks + 1, y_sweep, 0)

    def x_back(b, carry):
        n0 = pl.multiple_of(8 * b, 8)
        gates = [gate_x[g, pl.ds(n0, 8), :] for g in range(8)]
        here = [nat[c, pl.ds(n0, 8), :] for c in range(4)]
        cells = [[roll(v, 1) for v in here], here, [roll(v, -1) for v in here], [roll(v, -2) for v in here]]
        back = []
        for c in range(4):
            value = get(cot, (c,), pl.ds(n0, 8)) + get(d_mix, (), pl.ds(4 * n0 + Y_ORDER[c], 8, stride=4))
            value = value + get(face, (4 + c,), pl.ds(n0 - 1, 8)) - get(face, (c,), pl.ds(n0, 8))
            value = value + get(face, (8 + c,), pl.ds(n0 - 2, 8)) - get(face, (12 + c,), pl.ds(n0 - 3, 8))
            back.append(value)
        cots = [courant * (roll(v, -1) - v) for v in back]
        d_gates, minus_below, to_here, to_above, minus_above2 = flux_back(cells, gates, cots)

        def load(hi_ref, lo_ref):
            def of(pair):
                at = pl.ds(pl.multiple_of(256 * b + 64 * pair, 64), 64)
                return hi_ref[at, :], lo_ref[at, :]
            return of

        d_first = limiter_back(gates, d_gates, load(h1_hi, h1_lo), load(h2_hi, h2_lo))
        left_side, right_side = [], []
        for line in range(8):
            at = pl.ds(pl.multiple_of(128 * b + 16 * line, 16), 16)
            left_side.append(rows(t_hi[at, :], t_lo[at, :], ones))
            at = slice(32 * (line % 2), 32 * (line % 2) + 32)
            hi, lo = [v[at] for v in d_first[line // 2]]
            right_side.append(rows(hi, lo))
            put(zi, (), pl.ds(16 * line, 16), dot(w_xt[...], rows(hi, lo, hi)))
        acc_x[...] += dot_nt(lanes(*left_side), lanes(*right_side))
        for c in range(4):
            parts = [get(zi, (), pl.ds(4 * s + c, 8, stride=16)) for s in range(4)]
            value = back[c] + to_here[c] + parts[1] + roll(parts[0] - minus_below[c], -1)
            value = value + roll(to_above[c] + parts[2], 1) + roll(parts[3] - minus_above2[c], 2)
            out_nat[c, pl.ds(pl.multiple_of(n0 - 8, 8), 8), :] = value
        return carry

    lax.fori_loop(1, blocks + 1, x_back, 0)

    g_density[0] = out_nat[0].T
    g_momentum[0, 0] = out_nat[1].T
    g_momentum[0, 1] = out_nat[2].T
    g_tracer[0] = out_nat[3].T

    def index(shape, axis):
        return lax.broadcasted_iota(jnp.int32, shape, axis)

    def indicator(condition):
        return jnp.where(condition, 1.0, 0.0).astype(F32)

    r, k = index((24, 48), 0), index((24, 48), 1)
    pick = jnp.where(k < 32, k % 16, jnp.where(k == 32, 16, -1))
    first = exact(indicator(r == pick), acc_x[...])
    r, k = index((32, 64), 0), index((32, 64), 1)
    by_unit = exact(indicator(r == k % 32), first, nt=True)
    first = jnp.zeros((24, 256), F32)
    r, k = index((80, 256), 0), index((80, 256), 1)
    distance = (r // 4) % 8 - (k // 32) % 4
    for s in range(4):
        masked = jnp.where(jnp.logical_and(r < 64, distance == s), acc_y[...], 0.0)
        rr, kk = index((24, 80), 0), index((24, 80), 1)
        first = first + exact(indicator(jnp.logical_and(rr == 4 * s + kk % 4, kk < 64)), masked)
    masked = jnp.where(r == 64, acc_y[...], 0.0)
    rr, kk = index((24, 80), 0), index((24, 80), 1)
    first = first + exact(indicator(jnp.logical_and(rr == 16, kk == 64)), masked)
    r, k = index((32, 256), 0), index((32, 256), 1)
    by_unit = by_unit + exact(indicator(r == k % 32), first, nt=True)
    r, k = index((24, 128), 0), index((24, 128), 1)
    total = exact(by_unit, indicator(jnp.logical_and(k == r + 64, r <= 16)))
    r, k = index((32, 64), 0), index((32, 64), 1)
    summed = exact(indicator(r == k % 32), acc_m[...])
    r, k = index((80, 128), 0), index((80, 128), 1)
    place = jnp.where(r < 64, r % 32, jnp.where(r == 64, 32, -1))
    total = total + exact(summed, indicator(k == place))
    r, k = index((32, 144), 0), index((32, 144), 1)
    same = jnp.logical_or(k >= 128, (r // 8) % 2 == (k // 32) % 2)
    masked = jnp.where(same, acc_o[...], 0.0)
    r, k = index((8, 32), 0), index((8, 32), 1)
    summed = exact(indicator(r == k % 8), masked)
    r, k = index((144, 128), 0), index((144, 128), 1)
    place = jnp.where(r < 128, r % 32, jnp.where(r == 128, 32, -1))
    packed[0:32, :] = total
    packed[32:40, :] = exact(summed, indicator(k == place))


def weight_blocks(w_in, b_in, w_mid, b_mid, w_out, b_out):
    def parts_of(v):
        hi = lax.reduce_precision(v, 8, 7)
        mid = lax.reduce_precision(v - hi, 8, 7)
        return hi, mid, lax.reduce_precision(v - hi - mid, 8, 7)

    def triple(grow, v):
        hi, mid, _ = parts_of(v)
        return jnp.concatenate([grow(hi), grow(hi), grow(mid)], 1)

    def sixfold(grow, v, bias, count):
        hi, mid, low = parts_of(v)
        columns = jnp.stack([jnp.tile(part, count) for part in parts_of(bias)], 1)
        columns = jnp.pad(columns, ((0, 0), (0, 13)))
        hi, mid, low = grow(hi), grow(mid), grow(low)
        return jnp.concatenate([hi, hi, hi, mid, mid, low, columns], 1)

    def grow_y(v):
        shifts = v.reshape(32, 4, 4)
        lines = [jnp.pad(shifts, ((0, 0), (k, 4 - k), (0, 0))) for k in range(4)]
        return jnp.stack(lines, 0).reshape(128, 32)

    def grow_pair(v):
        eye = jnp.eye(2, dtype=F32)
        return (eye[:, None, :, None] * v[None, :, None, :]).reshape(2 * v.shape[0], 2 * v.shape[1])

    def same(v):
        return v

    w_x = sixfold(same, w_in, b_in, 1)
    w_y = sixfold(grow_y, w_in, b_in, 4)
    w_m = sixfold(same, w_mid, b_mid, 1)
    w_o = sixfold(same, w_out, b_out, 1)
    w_ot = triple(grow_pair, w_out.T)
    w_mt = triple(grow_pair, w_mid.T)
    w_xt = triple(same, w_in.T)
    w_yt = triple(lambda v: grow_y(v).T, w_in)
    return [v.astype(BF16) for v in (w_x, w_y, w_m, w_o, w_ot, w_mt, w_xt, w_yt)]


def ring_size(mesh):
    return mesh.shape["tx"] * mesh.shape["ty"]


def make_body(size):
    def body(density, momentum, tracer, cotangent, w_in, b_in, w_mid, b_mid, w_out, b_out):
        own, width = density.shape[2], density.shape[1]
        states = jnp.concatenate([density[:, None], momentum, tracer[:, None], cotangent], 1)[0]
        low = jnp.swapaxes(states[:, :, :HALO], 1, 2)
        high = jnp.swapaxes(states[:, :, own - HALO :], 1, 2)
        from_right = lax.ppermute(low, RING, [((i + 1) % size, i) for i in range(size)])
        from_left = lax.ppermute(high, RING, [(i, (i + 1) % size) for i in range(size)])
        halo = jnp.concatenate([from_right, from_left], 1)
        weights = weight_blocks(w_in, b_in, w_mid, b_mid, w_out, b_out)
        extra = own + 16
        lines = own + 8
        out = pl.pallas_call(
            kernel,
            out_shape=(
                jax.ShapeDtypeStruct(density.shape, F32),
                jax.ShapeDtypeStruct(momentum.shape, F32),
                jax.ShapeDtypeStruct(tracer.shape, F32),
                jax.ShapeDtypeStruct((40, 128), F32),
            ),
            in_specs=[pl.BlockSpec(memory_space=pltpu.VMEM)] * 13,
            out_specs=tuple([pl.BlockSpec(memory_space=pltpu.VMEM)] * 4),
            scratch_shapes=[
                pltpu.VMEM((4, lines, width), F32),
                pltpu.VMEM((4, 2, extra, 128), F32),
                pltpu.VMEM((4, 2, extra, 128), F32),
                pltpu.VMEM((4 * extra, width), BF16),
                pltpu.VMEM((4 * extra, width), BF16),
                pltpu.VMEM((4 * extra, width), BF16),
                pltpu.VMEM((32 * lines, width), BF16),
                pltpu.VMEM((32 * lines, width), BF16),
                pltpu.VMEM((32 * lines, width), BF16),
                pltpu.VMEM((32 * lines, width), BF16),
                pltpu.VMEM((16 * lines, width), BF16),
                pltpu.VMEM((16 * lines, width), BF16),
                pltpu.VMEM((8, lines, width), F32),
                pltpu.VMEM((16, 2, extra, 128), F32),
                pltpu.VMEM((2, 4 * extra, 128), F32),
                pltpu.VMEM((4, own, width), F32),
                pltpu.VMEM((2, 128, 128), F32),
                pltpu.VMEM((2, 64, 128), F32),
                pltpu.VMEM((2, 64, 128), F32),
                pltpu.VMEM((2, 32, 128), F32),
                pltpu.VMEM((2, 128, 128), F32),
                pltpu.VMEM((48, 64), F32),
                pltpu.VMEM((80, 256), F32),
                pltpu.VMEM((64, 80), F32),
                pltpu.VMEM((32, 144), F32),
            ],
            compiler_params=pltpu.CompilerParams(vmem_limit_bytes=60 * 1024 * 1024),
        )(density, momentum, tracer, cotangent, halo, *weights)
        total = lax.psum(out[3], ("traj", "tx", "ty"))
        return (
            out[0],
            out[1],
            out[2],
            total[0:32, 64:80],
            total[0:32, 80],
            total[0:32, 0:32],
            total[0:32, 32],
            total[32:40, 0:32],
            total[32:40, 32],
        )

    return body


def solution(mesh):
    in_specs = (
        P("traj", None, ("tx", "ty")),
        P("traj", None, None, ("tx", "ty")),
        P("traj", None, ("tx", "ty")),
        P("traj", None, None, ("tx", "ty")),
        P(), P(), P(), P(), P(), P(),
    )
    out_specs = (
        P("traj", None, ("tx", "ty")),
        P("traj", None, None, ("tx", "ty")),
        P("traj", None, ("tx", "ty")),
        P(), P(), P(), P(), P(), P(),
    )
    return jax.shard_map(
        make_body(ring_size(mesh)), mesh=mesh, in_specs=in_specs, out_specs=out_specs, check_vma=False
    )
```

profile of v0, /device:TPU:0, one launch (start us, length us, event | category | flops | bytes accessed | tf_op | source)
XLA Modules:
  0.0 158.6 jit_solution(7255188020034691127)
XLA Ops:
  0.7 1.3 copy.117
  2.1 0.8 copy-done
  3.0 0.8 copy-done.1
  4.0 1.7 %collective-permute-start.1 = (f32[8,4,256]{2,1,0:T(4,128)S(1)}, f32[8,4,256]{2,1,0:T(4,128)S(1)}, u32[]{:S(2)}, u32[]{:S(2)}) collective-permute-start(f32[8,4,256]{2,1,0:T(4,128)S(1)} %get-tuple-element.56), channel_id=1, source_target_pairs={{0,1},{1,2},{2,3},{3,4},{4,5},{5,6},{6,7},{7,8},{8,9},{9,10},{10,1... | collective-permute-start | bytes 98312 | tf_op jit(solution)/shard_map/ppermute | solution.py:440
  5.7 7.5 %collective-permute-start = (f32[8,4,256]{2,1,0:T(4,128)S(1)}, f32[8,4,256]{2,1,0:T(4,128)S(1)}, u32[]{:S(2)}, u32[]{:S(2)}) collective-permute-start(f32[8,4,256]{2,1,0:T(4,128)S(1)} %get-tuple-element.55), channel_id=1, source_target_pairs={{1,0},{2,1},{3,2},{4,3},{5,4},{6,5},{7,6},{8,7},{9,8},{10,9},{11,1... | collective-permute-start | bytes 98312 | tf_op jit(solution)/shard_map/ppermute | solution.py:439
  13.3 0.7 copy-done.5
  14.0 0.7 copy-done.4
  14.8 0.6 copy-done.6
  17.0 0.6 copy-done.8
  19.0 0.7 pad_maximum_fusion.4.w_ot
  19.7 0.7 pad_maximum_fusion.2.w_mt
  20.4 0.7 pad_maximum_fusion.5.w_xt
  21.0 0.6 pad_maximum_fusion.3.w_yt
  21.9 0.7 copy.141.w_y
  22.7 0.7 concatenate.40.w_x
  23.4 0.7 concatenate.42.w_m
  24.1 0.7 concatenate.43.w_o
  24.8 0.6 pad_maximum_fusion.halo
  25.4 66.3 %shard_map.169 = (f32[1,256,128]{2,1,0:T(8,128)}, f32[1,2,256,128]{3,2,1,0:T(8,128)}, f32[1,256,128]{2,1,0:T(8,128)}, f32[40,128]{1,0:T(8,128)}) custom-call(f32[1,256,128]{2,1,0:T(8,128)} %density.1, f32[1,2,256,128]{3,2,1,0:T(8,128)} %momentum.1, f32[1,256,128]{2,1,0:T(8,128)} %tracer.1, f32[1,4,256,128]{3,2,1,0:T(8,128)} %cotangent.1, ...), custom_call_target="tpu_custom_call" | custom-call | tf_op jit(solution)/shard_map/pallas_call | solution.py:445
  91.7 63.6 %psum.7 = f32[40,128]{1,0:T(8,128)S(1)} all-reduce(f32[40,128]{1,0:T(8,128)} %get-tuple-element.16), channel_id=1, replica_groups=mesh['traj'=4,'tx'=8,'ty'=4] {'traj','tx','ty'}, use_global_device_ids=true, to_apply=%region_0.1 | all-reduce | flops 5120 | bytes 40960 | tf_op jit(solution)/shard_map/psum | solution.py:484
  155.4 0.7 slice_reduce_fusion
  156.1 0.6 slice.36
  157.3 0.7 slice_reduce_fusion.2
  157.9 0.7 copy.142
  (84 shorter events, 4.5 us)
Async XLA Ops:
  0.6 1.3 copy-start.2
  1.9 1.0 copy-start
  2.9 0.9 copy-start.1
  4.0 9.2 %copy-start.3 = (f32[32,16]{0,1:T(8,128)S(1)}, f32[32,16]{0,1:T(8,128)}, u32[]{:S(2)}) copy-start(f32[32,16]{0,1:T(8,128)} %param.14) | copy-start | bytes 6148
  4.0 20.8 %collective-permute-start.1 = (f32[8,4,256]{2,1,0:T(4,128)S(1)}, f32[8,4,256]{2,1,0:T(4,128)S(1)}, u32[]{:S(2)}, u32[]{:S(2)}) collective-permute-start(f32[8,4,256]{2,1,0:T(4,128)S(1)} %get-tuple-element.56), channel_id=1, source_target_pairs={{0,1},{1,2},{2,3},{3,4},{4,5},{5,6},{6,7},{7,8},{8,9},{9,10},{10,1... | collective-permute-start | bytes 98312 | tf_op jit(solution)/shard_map/ppermute | solution.py:440
  5.7 19.1 %collective-permute-start = (f32[8,4,256]{2,1,0:T(4,128)S(1)}, f32[8,4,256]{2,1,0:T(4,128)S(1)}, u32[]{:S(2)}, u32[]{:S(2)}) collective-permute-start(f32[8,4,256]{2,1,0:T(4,128)S(1)} %get-tuple-element.55), channel_id=1, source_target_pairs={{1,0},{2,1},{3,2},{4,3},{5,4},{6,5},{7,6},{8,7},{9,8},{10,9},{11,1... | collective-permute-start | bytes 98312 | tf_op jit(solution)/shard_map/ppermute | solution.py:439
  13.3 0.7 copy-start.5
  14.0 0.7 copy-start.4
  14.7 0.7 copy-start.6
  16.3 0.7 copy-start.7
  17.0 0.7 copy-start.8
where the time goes:
time: 159 us
  Pallas kernels  66.3 us (42%)
  blocking collectives  63.6 us (40%)
  local copies, waits for them, and re-layouts  14.9 us (9%)
  starting transfers between devices  9.12 us (6%)
  other arithmetic  3.87 us (2%)
    pallas_call x1, Pallas kernels, body(): pl.pallas_call(kernel, out_shape=(jax.ShapeDtypeStruct(density.shape, F32...  66.3 us
    psum x1, blocking collectives, body(): total = lax.psum(out[3], ('traj', 'tx', 'ty'))  63.6 us
    ppermute x1, starting transfers between devices, body(): lax.ppermute(low, RING, [((i + 1) % size, i) for i in range(size)])  7.45 us
    unnamed x31, local copies, waits for them, and re-layouts  7.23 us
  transfers between devices with their start and end apart: 2, of which 0 were waited for; matrix products, arithmetic and copies ran while one was open for 5% of the time, Pallas kernels for 0%

commit v1 on v0

--- a/solution.py
+++ b/solution.py
@@ -1,3 +1,5 @@
+import functools
+
 import jax
 import jax.numpy as jnp
 from jax import lax
@@ -133,20 +135,93 @@
     return d_gates, minus_below, to_here, to_above, minus_above2
 
 
+def index(shape, axis):
+    return lax.broadcasted_iota(jnp.int32, shape, axis)
+
+
+def indicator(condition, dtype=F32):
+    return jnp.where(condition, 1.0, 0.0).astype(F32).astype(dtype)
+
+
+def fill_weights(given, filled):
+    w_in, b_in, w_mid, b_mid, w_out, b_out = [ref[...] for ref in given]
+    w_x, w_y, w_m, w_o, w_ot, w_mt, w_xt, w_yt = filled
+
+    def bias_columns(bias, count, depth):
+        parts = split3(jnp.broadcast_to(bias, (16, count)))
+        r = index((16, count), 0)
+        stacked = jnp.zeros((16, count), F32)
+        for at in range(3):
+            stacked = jnp.where(r == at, parts[at].astype(F32), stacked)
+        below = jnp.zeros((depth, count), BF16)
+        unit = indicator(index((count, count), 0) == index((count, count), 1), BF16)
+        return dot_nt(unit, rows(below, stacked.astype(BF16)))
+
+    def spread(parts, owners, block, columns, offset=0):
+        count = parts[0].shape[1]
+        r, k = index((count, columns), 0), index((count, columns), 1)
+        total = None
+        for at, part in enumerate(parts):
+            inside = jnp.logical_and(k >= owners[at][0] * block, k < owners[at][1] * block)
+            where = jnp.logical_and(inside, k % block == r + offset)
+            piece = dot(part, indicator(where, BF16))
+            total = piece if total is None else total + piece
+        return total
+
+    sixfold = ((0, 3), (3, 5), (5, 6))
+    threefold = ((0, 2), (2, 3))
+    for ref, weight, bias in ((w_x, w_in, b_in), (w_m, w_mid, b_mid), (w_o, w_out, b_out)):
+        units, count = weight.shape
+        value = spread(split3(weight), sixfold, count, 6 * count + 16)
+        ref[...] = (value + bias_columns(bias, units, 6 * count)).astype(BF16)
+    in_parts = split3(w_in)
+    in_bias = bias_columns(b_in, 32, 192)
+    for face in range(4):
+        value = spread(in_parts, sixfold, 32, 208, 4 * face) + in_bias
+        w_y[32 * face : 32 * face + 32, :] = value.astype(BF16)
+
+    def turned(weight, lines):
+        units = weight.shape[1]
+        r, k = index((lines * units, units), 0), index((lines * units, units), 1)
+        chosen = indicator(r % units == k, BF16)
+        return [dot_nt(chosen, part).astype(BF16) for part in split(weight)]
+
+    for ref, weight in ((w_ot, w_out), (w_mt, w_mid)):
+        gates, units = weight.shape
+        parts = turned(weight, 2)
+        shape = (2 * units, 6 * gates)
+        r, k = index(shape, 0), index(shape, 1)
+        value = spread(parts, ((0, 4), (4, 6)), gates, 6 * gates)
+        ref[...] = jnp.where((k // gates) % 2 == r // units, value, 0.0).astype(BF16)
+    w_xt[...] = spread(turned(w_in, 1), threefold, 32, 96).astype(BF16)
+    total = None
+    for face in range(4):
+        r, k = index((32, 16), 0), index((32, 16), 1)
+        chosen = indicator(r == k + 4 * face, BF16)
+        parts = [dot_nt(chosen, part).astype(BF16) for part in split(w_in)]
+        value = spread(parts, threefold, 128, 384, 32 * face)
+        total = value if total is None else total + value
+    w_yt[...] = total.astype(BF16)
+
+
 def kernel(
     density, momentum, tracer, cotangent, halo,
-    w_x, w_y, w_m, w_o, w_ot, w_mt, w_xt, w_yt,
+    w_in, b_in, w_mid, b_mid, w_out, b_out,
     g_density, g_momentum, g_tracer, packed,
     nat, cot, mid, mid_hi, mid_lo, mid_lo2,
     h1_hi, h1_lo, h2_hi, h2_lo, t_hi, t_lo, gate_x,
     face, d_mix, out_nat,
     xi, gi, di, mi, zi,
     acc_x, acc_y, acc_m, acc_o,
+    w_x, w_y, w_m, w_o, w_ot, w_mt, w_xt, w_yt,
 ):
     width = nat.shape[2]
     own = density.shape[2]
     blocks = own // 8
     ones = jnp.ones((16, width), BF16)
+    fill_weights(
+        (w_in, b_in, w_mid, b_mid, w_out, b_out), (w_x, w_y, w_m, w_o, w_ot, w_mt, w_xt, w_yt)
+    )
 
     for c in range(4):
         if c == 0:
@@ -345,92 +420,104 @@
     g_momentum[0, 1] = out_nat[2].T
     g_tracer[0] = out_nat[3].T
 
-    def index(shape, axis):
-        return lax.broadcasted_iota(jnp.int32, shape, axis)
-
-    def indicator(condition):
-        return jnp.where(condition, 1.0, 0.0).astype(F32)
-
     r, k = index((24, 48), 0), index((24, 48), 1)
     pick = jnp.where(k < 32, k % 16, jnp.where(k == 32, 16, -1))
-    first = exact(indicator(r == pick), acc_x[...])
-    r, k = index((32, 64), 0), index((32, 64), 1)
-    by_unit = exact(indicator(r == k % 32), first, nt=True)
-    first = jnp.zeros((24, 256), F32)
+    first_x = exact(indicator(r == pick), acc_x[...])
     r, k = index((80, 256), 0), index((80, 256), 1)
     distance = (r // 4) % 8 - (k // 32) % 4
+    rr, kk = index((24, 80), 0), index((24, 80), 1)
+    masked = jnp.where(r == 64, acc_y[...], 0.0)
+    first_y = exact(indicator(jnp.logical_and(rr == 16, kk == 64)), masked)
     for s in range(4):
         masked = jnp.where(jnp.logical_and(r < 64, distance == s), acc_y[...], 0.0)
-        rr, kk = index((24, 80), 0), index((24, 80), 1)
-        first = first + exact(indicator(jnp.logical_and(rr == 4 * s + kk % 4, kk < 64)), masked)
-    masked = jnp.where(r == 64, acc_y[...], 0.0)
-    rr, kk = index((24, 80), 0), index((24, 80), 1)
-    first = first + exact(indicator(jnp.logical_and(rr == 16, kk == 64)), masked)
-    r, k = index((32, 256), 0), index((32, 256), 1)
-    by_unit = by_unit + exact(indicator(r == k % 32), first, nt=True)
+        first_y = first_y + exact(indicator(jnp.logical_and(rr == 4 * s + kk % 4, kk < 64)), masked)
+
+    def by_unit(shape, axis):
+        return indicator(index(shape, axis) % 32 == index(shape, 1 - axis))
+
+    first = exact(by_unit((32, 64), 1), first_x, nt=True) + exact(by_unit((32, 256), 1), first_y, nt=True)
+    first_bias = exact(first_x, by_unit((64, 32), 0)) + exact(first_y, by_unit((256, 32), 0))
     r, k = index((24, 128), 0), index((24, 128), 1)
-    total = exact(by_unit, indicator(jnp.logical_and(k == r + 64, r <= 16)))
-    r, k = index((32, 64), 0), index((32, 64), 1)
-    summed = exact(indicator(r == k % 32), acc_m[...])
+    total = exact(first, indicator(jnp.logical_and(k == r + 64, r < 16)))
     r, k = index((80, 128), 0), index((80, 128), 1)
-    place = jnp.where(r < 64, r % 32, jnp.where(r == 64, 32, -1))
-    total = total + exact(summed, indicator(k == place))
+    total = total + exact(exact(by_unit((32, 64), 1), acc_m[...]), indicator(jnp.logical_and(r % 32 == k, r < 64)))
+    second_bias = exact(exact(indicator(index((8, 80), 1) == 64), acc_m[...], nt=True), by_unit((64, 32), 0))
     r, k = index((32, 144), 0), index((32, 144), 1)
-    same = jnp.logical_or(k >= 128, (r // 8) % 2 == (k // 32) % 2)
-    masked = jnp.where(same, acc_o[...], 0.0)
+    masked = jnp.where(jnp.logical_and(k < 128, (r // 8) % 2 == (k // 32) % 2), acc_o[...], 0.0)
     r, k = index((8, 32), 0), index((8, 32), 1)
     summed = exact(indicator(r == k % 8), masked)
     r, k = index((144, 128), 0), index((144, 128), 1)
-    place = jnp.where(r < 128, r % 32, jnp.where(r == 128, 32, -1))
     packed[0:32, :] = total
-    packed[32:40, :] = exact(summed, indicator(k == place))
-
-
-def weight_blocks(w_in, b_in, w_mid, b_mid, w_out, b_out):
-    def parts_of(v):
-        hi = lax.reduce_precision(v, 8, 7)
-        mid = lax.reduce_precision(v - hi, 8, 7)
-        return hi, mid, lax.reduce_precision(v - hi - mid, 8, 7)
-
-    def triple(grow, v):
-        hi, mid, _ = parts_of(v)
-        return jnp.concatenate([grow(hi), grow(hi), grow(mid)], 1)
-
-    def sixfold(grow, v, bias, count):
-        hi, mid, low = parts_of(v)
-        columns = jnp.stack([jnp.tile(part, count) for part in parts_of(bias)], 1)
-        columns = jnp.pad(columns, ((0, 0), (0, 13)))
-        hi, mid, low = grow(hi), grow(mid), grow(low)
-        return jnp.concatenate([hi, hi, hi, mid, mid, low, columns], 1)
-
-    def grow_y(v):
-        shifts = v.reshape(32, 4, 4)
-        lines = [jnp.pad(shifts, ((0, 0), (k, 4 - k), (0, 0))) for k in range(4)]
-        return jnp.stack(lines, 0).reshape(128, 32)
-
-    def grow_pair(v):
-        eye = jnp.eye(2, dtype=F32)
-        return (eye[:, None, :, None] * v[None, :, None, :]).reshape(2 * v.shape[0], 2 * v.shape[1])
-
-    def same(v):
-        return v
-
-    w_x = sixfold(same, w_in, b_in, 1)
-    w_y = sixfold(grow_y, w_in, b_in, 4)
-    w_m = sixfold(same, w_mid, b_mid, 1)
-    w_o = sixfold(same, w_out, b_out, 1)
-    w_ot = triple(grow_pair, w_out.T)
-    w_mt = triple(grow_pair, w_mid.T)
-    w_xt = triple(same, w_in.T)
-    w_yt = triple(lambda v: grow_y(v).T, w_in)
-    return [v.astype(BF16) for v in (w_x, w_y, w_m, w_o, w_ot, w_mt, w_xt, w_yt)]
+    packed[32:40, :] = exact(summed, indicator(jnp.logical_and(r % 32 == k, r < 128)))
+    out_bias = exact(indicator(index((8, 144), 1) == 128), acc_o[...], nt=True)
+    r, k = index((32, 128), 0), index((32, 128), 1)
+    out_bias = exact(out_bias, indicator(r % 8 == k))
+    r, k = index((32, 128), 0), index((32, 128), 1)
+    wide = indicator(r == k)
+    first_bias = exact(first_bias[16:24], wide)
+    second_bias = exact(second_bias, wide)
+    r = index((8, 128), 0)
+    first_bias = jnp.broadcast_to(first_bias[0:1], (8, 128))
+    packed[40:48, :] = jnp.where(
+        r == 0, first_bias, jnp.where(r == 1, second_bias, jnp.where(r == 2, out_bias, 0.0))
+    )
+
+
+GROUPS = ("traj", "ty", "tx")
+
+
+def reduce_kernel(sizes, mine, total, *scratch):
+    count = len(sizes)
+    slots, sends, receives = scratch[:count], scratch[count : 2 * count], scratch[2 * count :]
+    mesh_ids = pl.DeviceIdType.MESH
+    barrier = pltpu.get_barrier_semaphore()
+    for axis, size in zip(GROUPS, sizes):
+        here = lax.axis_index(axis)
+        for step in range(1, size):
+            peer = lax.rem(here + step, size)
+            pl.semaphore_signal(barrier, inc=1, device_id={axis: peer}, device_id_type=mesh_ids)
+    pl.semaphore_wait(barrier, sum(sizes) - count)
+    value = mine[...]
+    for at, (axis, size) in enumerate(zip(GROUPS, sizes)):
+        here = lax.axis_index(axis)
+        slots[at][here] = value
+        copies = []
+        for step in range(1, size):
+            peer = lax.rem(here + step, size)
+            copies.append(
+                pltpu.make_async_remote_copy(
+                    src_ref=slots[at].at[here],
+                    dst_ref=slots[at].at[here],
+                    send_sem=sends[at].at[step],
+                    recv_sem=receives[at].at[step],
+                    device_id={axis: peer},
+                    device_id_type=mesh_ids,
+                )
+            )
+        for copy in copies:
+            copy.start()
+        for copy in copies:
+            copy.wait()
+        value = slots[at][0]
+        for other in range(1, size):
+            value = value + slots[at][other]
+    total[...] = value
+
+
+def unpack_kernel(total, g_w_in, g_b_in, g_w_mid, g_b_mid, g_w_out, g_b_out):
+    g_w_in[...] = total[0:32, 64:80]
+    g_b_in[...] = total[40:41, 0:32]
+    g_w_mid[...] = total[0:32, 0:32]
+    g_b_mid[...] = total[41:42, 0:32]
+    g_w_out[...] = total[32:40, 0:32]
+    g_b_out[...] = total[42:43, 0:8]
 
 
 def ring_size(mesh):
     return mesh.shape["tx"] * mesh.shape["ty"]
 
 
-def make_body(size):
+def make_body(size, sizes):
     def body(density, momentum, tracer, cotangent, w_in, b_in, w_mid, b_mid, w_out, b_out):
         own, width = density.shape[2], density.shape[1]
         states = jnp.concatenate([density[:, None], momentum, tracer[:, None], cotangent], 1)[0]
@@ -439,7 +526,8 @@
         from_right = lax.ppermute(low, RING, [((i + 1) % size, i) for i in range(size)])
         from_left = lax.ppermute(high, RING, [(i, (i + 1) % size) for i in range(size)])
         halo = jnp.concatenate([from_right, from_left], 1)
-        weights = weight_blocks(w_in, b_in, w_mid, b_mid, w_out, b_out)
+        biases = [b.reshape(1, -1) for b in (b_in, b_mid, b_out)]
+        weights = (w_in, biases[0], w_mid, biases[1], w_out, biases[2])
         extra = own + 16
         lines = own + 8
         out = pl.pallas_call(
@@ -448,9 +536,9 @@
                 jax.ShapeDtypeStruct(density.shape, F32),
                 jax.ShapeDtypeStruct(momentum.shape, F32),
                 jax.ShapeDtypeStruct(tracer.shape, F32),
-                jax.ShapeDtypeStruct((40, 128), F32),
+                jax.ShapeDtypeStruct((48, 128), F32),
             ),
-            in_specs=[pl.BlockSpec(memory_space=pltpu.VMEM)] * 13,
+            in_specs=[pl.BlockSpec(memory_space=pltpu.VMEM)] * 11,
             out_specs=tuple([pl.BlockSpec(memory_space=pltpu.VMEM)] * 4),
             scratch_shapes=[
                 pltpu.VMEM((4, lines, width), F32),
@@ -478,20 +566,44 @@
                 pltpu.VMEM((80, 256), F32),
                 pltpu.VMEM((64, 80), F32),
                 pltpu.VMEM((32, 144), F32),
+                pltpu.VMEM((32, 112), BF16),
+                pltpu.VMEM((128, 208), BF16),
+                pltpu.VMEM((32, 208), BF16),
+                pltpu.VMEM((8, 208), BF16),
+                pltpu.VMEM((64, 48), BF16),
+                pltpu.VMEM((64, 192), BF16),
+                pltpu.VMEM((16, 96), BF16),
+                pltpu.VMEM((32, 384), BF16),
             ],
             compiler_params=pltpu.CompilerParams(vmem_limit_bytes=60 * 1024 * 1024),
         )(density, momentum, tracer, cotangent, halo, *weights)
-        total = lax.psum(out[3], ("traj", "tx", "ty"))
+        in_vmem = pl.BlockSpec(memory_space=pltpu.VMEM)
+        shape = (48, 128)
+        total = pl.pallas_call(
+            functools.partial(reduce_kernel, sizes),
+            out_shape=jax.ShapeDtypeStruct(shape, F32),
+            in_specs=[in_vmem],
+            out_specs=in_vmem,
+            scratch_shapes=[pltpu.VMEM((n,) + shape, F32) for n in sizes]
+            + [pltpu.SemaphoreType.DMA((n,)) for n in sizes] * 2,
+            compiler_params=pltpu.CompilerParams(collective_id=0, has_side_effects=True),
+        )(out[3])
+        totals = pl.pallas_call(
+            unpack_kernel,
+            out_shape=tuple(jax.ShapeDtypeStruct(w.shape, F32) for w in weights),
+            in_specs=[in_vmem],
+            out_specs=tuple([in_vmem] * 6),
+        )(total)
         return (
             out[0],
             out[1],
             out[2],
-            total[0:32, 64:80],
-            total[0:32, 80],
-            total[0:32, 0:32],
-            total[0:32, 32],
-            total[32:40, 0:32],
-            total[32:40, 32],
+            totals[0],
+            totals[1].reshape(-1),
+            totals[2],
+            totals[3].reshape(-1),
+            totals[4],
+            totals[5].reshape(-1),
         )
 
     return body
@@ -512,5 +624,5 @@
         P(), P(), P(), P(), P(), P(),
     )
     return jax.shard_map(
-        make_body(ring_size(mesh)), mesh=mesh, in_specs=in_specs, out_specs=out_specs, check_vma=False
+        make_body(ring_size(mesh), tuple(mesh.shape[axis] for axis in GROUPS)), mesh=mesh, in_specs=in_specs, out_specs=out_specs, check_vma=False
     )

time: 159 us -> 109 us (0.69)
  blocking collectives: 63.6 us -> 0 us
  Pallas kernels: 66.3 us -> 83 us
  local copies, waits for them, and re-layouts: 14.9 us -> 5.25 us
  waiting for transfers between devices: 0.01 us -> 8.95 us
  other arithmetic: 3.87 us -> 0.72 us
    psum x1 -> x0, blocking collectives: 63.6 us -> none  [body(): total = lax.psum(out[3], ('traj', 'tx', 'ty'))]
    pallas_call x0 -> x2, Pallas kernels: none -> 15.7 us  [the longest x1 14.3 us: body(): pl.pallas_call(functools.partial(reduce_kernel, sizes), out_shape=jax.Sha...]
    ppermute x1, waiting for transfers between devices: 0.01 us -> 8.04 us  [body(): lax.ppermute(high, RING, [(i, (i + 1) % size) for i in range(size)])]
    concatenate x4 -> x0, local copies, waits for them, and re-layouts: 2.8 us -> none  [sixfold(): return jnp.concatenate([hi, hi, hi, mid, mid, low, columns], 1)]
    concatenate x5 -> x0, other arithmetic: 2.69 us -> none  [the longest x4 2.68 us: triple(): return jnp.concatenate([grow(hi), grow(hi), grow(mid)], 1)]
    slice x5 -> x0, local copies, waits for them, and re-layouts: 2.66 us -> none  [the longest x1 0.7 us: body(): total[0:32, 32]]
    unnamed x31 -> x14, local copies, waits for them, and re-layouts: 7.23 us -> 5.24 us
    ppermute x1, starting transfers between devices: 1.67 us -> 0.01 us  [body(): lax.ppermute(high, RING, [(i, (i + 1) % size) for i in range(size)])]
  transfers between devices with their start and end apart: 2 -> 2, of which waited for: 0 -> 2; matrix products, arithmetic and copies ran while one was open for 5% -> 1% of each run, Pallas kernels for 0% -> 0%
where the time goes in v1:
time: 109 us; the launch traced here: 108 us
  Pallas kernels  83 us (76%)
  starting transfers between devices  9.05 us (8%)
  waiting for transfers between devices  8.95 us (8%)
  local copies, waits for them, and re-layouts  5.25 us (5%)
    pallas_call x1, Pallas kernels, body(): pl.pallas_call(kernel, out_shape=(jax.ShapeDtypeStruct(density.shape, F32...  67.3 us
    pallas_call x1, Pallas kernels, body(): pl.pallas_call(functools.partial(reduce_kernel, sizes), out_shape=jax.Sha...  14.3 us
    ppermute x1, starting transfers between devices, body(): lax.ppermute(low, RING, [((i + 1) % size, i) for i in range(size)])  9.04 us
    ppermute x1, waiting for transfers between devices, body(): lax.ppermute(high, RING, [(i, (i + 1) % size) for i in range(size)])  8.04 us
    unnamed x14, local copies, waits for them, and re-layouts  5.24 us
  transfers between devices with their start and end apart: 2, of which 2 were waited for; matrix products, arithmetic and copies ran while one was open for 1% of the time, Pallas kernels for 0%

profile of v1, /device:TPU:0, one launch (start us, length us, event | category | flops | bytes accessed | tf_op | source)
XLA Modules:
  0.0 107.7 jit_solution(4003762372477424309)
XLA Ops:
  0.6 0.0 copy-start
  0.7 1.3 %copy.22 = f32[1,4,256,128]{2,3,1,0:T(8,128)S(1)} copy(f32[1,4,256,128]{3,2,1,0:T(8,128)} %cotangent.1) | data formatting | bytes 1048576 | tf_op args[3]
  1.9 0.0 copy-done
  2.0 0.0 copy-start.1
  2.0 0.1 copy.21
  2.1 0.8 copy-done.1
  2.9 0.0 copy-start.2
  2.9 0.1 copy.19
  3.0 0.8 copy-done.2
  3.8 0.1 copy.20
  3.9 0.1 maximum_bitcast_fusion
  3.9 0.0 copy-start.3
  4.0 9.0 %collective-permute-start = (f32[8,4,256]{2,1,0:T(4,128)S(1)}, f32[8,4,256]{2,1,0:T(4,128)S(1)}, u32[]{:S(2)}, u32[]{:S(2)}) collective-permute-start(f32[8,4,256]{2,1,0:T(4,128)S(1)} %get-tuple-element.38), channel_id=1, source_target_pairs={{1,0},{2,1},{3,2},{4,3},{5,4},{6,5},{7,6},{8,7},{9,8},{10,9},{11,1... | collective-permute-start | bytes 98312 | tf_op jit(solution)/shard_map/ppermute | solution.py:526
  13.0 0.0 collective-permute-start.1
  13.0 0.0 copy-done.3
  13.0 0.7 copy.23.w_in
  13.7 0.9 collective-permute-done
  14.6 8.0 %collective-permute-done.1 = f32[8,4,256]{2,1,0:T(4,128)S(1)} collective-permute-done((f32[8,4,256]{2,1,0:T(4,128)S(1)}, f32[8,4,256]{2,1,0:T(4,128)S(1)}, u32[]{:S(2)}, u32[]{:S(2)}) %collective-permute-start.1) | collective-permute-done | bytes 32800 | tf_op jit(solution)/shard_map/ppermute | solution.py:527
  22.7 0.6 pad_maximum_fusion.halo
  23.3 67.3 %shard_map.169 = (f32[1,256,128]{2,1,0:T(8,128)}, f32[1,2,256,128]{3,2,1,0:T(8,128)}, f32[1,256,128]{2,1,0:T(8,128)}, f32[48,128]{1,0:T(8,128)}) custom-call(f32[1,256,128]{2,1,0:T(8,128)} %density.1, f32[1,2,256,128]{3,2,1,0:T(8,128)} %momentum.1, f32[1,256,128]{2,1,0:T(8,128)} %tracer.1, f32[1,4,256,128]{3,2,1,0:T(8,128)} %cotangent.1, ...), custom_call_target="tpu_custom_call" | custom-call | tf_op jit(solution)/shard_map/pallas_call | solution.py:533
  90.6 14.3 %shard_map.170.total = f32[48,128]{1,0:T(8,128)} custom-call(f32[48,128]{1,0:T(8,128)} %get-tuple-element.22.mine), custom_call_target="tpu_custom_call" | custom-call | tf_op jit(solution)/shard_map/pallas_call | solution.py:582
  104.9 1.4 %shard_map.171 = (f32[32,16]{1,0:T(8,128)}, f32[1,32]{1,0:T(1,128)}, f32[32,32]{1,0:T(8,128)}, f32[1,32]{1,0:T(1,128)}, f32[8,32]{1,0:T(8,128)}, /*index=5*/f32[1,8]{1,0:T(1,128)}) custom-call(f32[48,128]{1,0:T(8,128)} %shard_map.170.total), custom_call_target="tpu_custom_call" | custom-call | tf_op jit(solution)/shard_map/pallas_call | solution.py:591
  106.3 1.4 %copy.24 = f32[32,16]{0,1:T(8,128)} copy(f32[32,16]{1,0:T(8,128)} %get-tuple-element.32) | data formatting | bytes 4096
  (1 shorter events, 0.0 us)
Async XLA Ops:
  0.6 1.3 %copy-start = (f32[1,2,256,128]{3,2,1,0:T(8,128)S(1)}, f32[1,2,256,128]{3,2,1,0:T(8,128)}, u32[]{:S(2)}) copy-start(f32[1,2,256,128]{3,2,1,0:T(8,128)} %momentum.1) | copy-start | bytes 786436
  2.0 0.9 copy-start.1
  2.9 0.9 copy-start.2
  3.9 9.1 %copy-start.3 = (f32[32,16]{0,1:T(8,128)S(1)}, f32[32,16]{0,1:T(8,128)}, u32[]{:S(2)}) copy-start(f32[32,16]{0,1:T(8,128)} %param.14) | copy-start | bytes 6148
  4.0 10.6 %collective-permute-start = (f32[8,4,256]{2,1,0:T(4,128)S(1)}, f32[8,4,256]{2,1,0:T(4,128)S(1)}, u32[]{:S(2)}, u32[]{:S(2)}) collective-permute-start(f32[8,4,256]{2,1,0:T(4,128)S(1)} %get-tuple-element.38), channel_id=1, source_target_pairs={{1,0},{2,1},{3,2},{4,3},{5,4},{6,5},{7,6},{8,7},{9,8},{10,9},{11,1... | collective-permute-start | bytes 98312 | tf_op jit(solution)/shard_map/ppermute | solution.py:526
  13.0 9.6 %collective-permute-start.1 = (f32[8,4,256]{2,1,0:T(4,128)S(1)}, f32[8,4,256]{2,1,0:T(4,128)S(1)}, u32[]{:S(2)}, u32[]{:S(2)}) collective-permute-start(f32[8,4,256]{2,1,0:T(4,128)S(1)} %get-tuple-element.39), channel_id=1, source_target_pairs={{0,1},{1,2},{2,3},{3,4},{4,5},{5,6},{6,7},{7,8},{8,9},{9,10},{10,1... | collective-permute-start | bytes 98312 | tf_op jit(solution)/shard_map/ppermute | solution.py:527

commit v2 on v1

--- a/solution.py
+++ b/solution.py
@@ -14,6 +14,7 @@
 HALO = 4
 RING = ("tx", "ty")
 Y_ORDER = (0, 2, 1, 3)
+STAGES = "bybybybyfbyfyfyfy"
 
 
 def split(x):
@@ -211,8 +212,8 @@
     nat, cot, mid, mid_hi, mid_lo, mid_lo2,
     h1_hi, h1_lo, h2_hi, h2_lo, t_hi, t_lo, gate_x,
     face, d_mix, out_nat,
-    xi, gi, di, mi, zi,
-    acc_x, acc_y, acc_m, acc_o,
+    xi, gi, gi_y, di, di_y, mi, zi,
+    acc_x, acc_y, acc_m, acc_o, acc_my, acc_oy,
     w_x, w_y, w_m, w_o, w_ot, w_mt, w_xt, w_yt,
 ):
     width = nat.shape[2]
@@ -232,6 +233,7 @@
             source = momentum[0, c - 1]
         nat[c, 8 : 8 + own, :] = source.T
         nat[c, 0:8, :] = halo[c]
+        nat[c, 8 + own : 16 + own, :] = halo[c]
         put(cot, (c,), pl.ds(8, own), cotangent[0, c].T)
         put(cot, (c,), pl.ds(0, 8), halo[4 + c])
         put(cot, (c,), pl.ds(8 + own, 8), halo[4 + c])
@@ -239,73 +241,84 @@
     acc_y[...] = jnp.zeros_like(acc_y)
     acc_m[...] = jnp.zeros_like(acc_m)
     acc_o[...] = jnp.zeros_like(acc_o)
-
-    def upper_layers(first):
-        first_parts = split3(first)
-        seconds, gate_rows = [], []
-        for line in range(4):
-            at = slice(32 * line, 32 * line + 32)
-            operand = six([part[at] for part in first_parts], ones)
-            second = split3(jnp.tanh(dot(w_m[...], operand)))
-            seconds.append(second)
-            gate_rows.append(jnp.tanh(dot(w_o[...], six(second, ones))))
-        return (
-            first_parts[0],
-            first_parts[1],
-            rows(*[v[0] for v in seconds]),
-            rows(*[v[1] for v in seconds]),
-            rows(*gate_rows),
-        )
-
-    def limiter_back(gates, d_gates, load_first, load_second):
+    acc_my[...] = jnp.zeros_like(acc_my)
+    acc_oy[...] = jnp.zeros_like(acc_oy)
+
+    def middle(pre):
+        firsts = [split3(jnp.tanh(v)) for v in pre]
+        return firsts, [dot(w_m[...], six(v, ones)) for v in firsts]
+
+    def output(pre):
+        seconds = [split3(jnp.tanh(v)) for v in pre]
+        return seconds, [dot(w_o[...], six(v, ones)) for v in seconds]
+
+    def natural_gates(pre, gi):
+        for line in range(8):
+            put(gi, (), pl.ds(8 * line, 8), jnp.tanh(pre[line]))
+        return [get(gi, (), pl.ds(g, 8, stride=8)) for g in range(8)]
+
+    def back_output(gates, d_gates, di, load_second):
         for g in range(8):
             put(di, (), pl.ds(g, 8, stride=8), d_gates[g] * (1.0 - gates[g] * gates[g]))
-        d_first, mid_lhs, mid_rhs, out_lhs, out_rhs = [], [], [], [], []
+        outs, pres = [], []
         for pair in range(4):
             o_hi, o_lo = split(get(di, (), pl.ds(16 * pair, 16)))
-            s_hi, s_lo = load_second(pair)
+            outs.append((o_hi, o_lo))
+            pres.append(dot(w_ot[...], rows(o_hi, o_lo, o_hi)))
+        return outs, pres
+
+    def back_through(pres, load, weight):
+        parts, nexts = [], []
+        for pair in range(4):
+            s_hi, s_lo = load(pair)
+            value = s_hi.astype(F32) + s_lo.astype(F32)
+            part = split(pres[pair] * (1.0 - value * value))
+            parts.append(part)
+            if weight is not None:
+                nexts.append(dot(weight[...], rows(part[0], part[1], part[0])))
+        return parts, nexts
+
+    def weight_sums(outs, d_second, load_first, load_second, acc_m, acc_o, valid):
+        mid_lhs, mid_rhs, out_lhs, out_rhs = [], [], [], []
+        for pair in range(4):
             f_hi, f_lo = load_first(pair)
-            second = s_hi.astype(F32) + s_lo.astype(F32)
-            d_second = dot(w_ot[...], rows(o_hi, o_lo, o_hi)) * (1.0 - second * second)
-            m_hi, m_lo = split(d_second)
-            first = f_hi.astype(F32) + f_lo.astype(F32)
-            d_one = dot(w_mt[...], rows(m_hi, m_lo, m_hi)) * (1.0 - first * first)
-            d_first.append(split(d_one))
             for line in range(2):
                 at = slice(32 * line, 32 * line + 32)
-                mid_lhs.append(rows(m_hi[at], m_lo[at]))
+                mid_lhs.append(rows(d_second[pair][0][at], d_second[pair][1][at]))
                 mid_rhs.append(rows(f_hi[at], f_lo[at], ones))
-            out_lhs.append(rows(o_hi, o_lo))
-            out_rhs.append(rows(s_hi, s_lo, ones))
-        acc_m[...] += dot_nt(lanes(*mid_lhs), lanes(*mid_rhs))
-        acc_o[...] += dot_nt(lanes(*out_lhs), lanes(*out_rhs))
-        return d_first
-
-    def x_forward(b, carry):
+            out_lhs.append(rows(*outs[pair]))
+            out_rhs.append(rows(*load_second(pair), ones))
+        acc_m[...] += jnp.where(valid, dot_nt(lanes(*mid_lhs), lanes(*mid_rhs)), 0.0)
+        acc_o[...] += jnp.where(valid, dot_nt(lanes(*out_lhs), lanes(*out_rhs)), 0.0)
+
+    def x_forward(b):
         n0 = pl.multiple_of(8 * b, 8)
         here = [nat[c, pl.ds(n0, 8), :] for c in range(4)]
         cells = [[roll(v, 1) for v in here], here, [roll(v, -1) for v in here], [roll(v, -2) for v in here]]
         for s in range(4):
             for c in range(4):
                 put(xi, (), pl.ds(4 * s + c, 8, stride=16), cells[s][c])
-        for q in range(2):
-            window = split3(get(xi, (), pl.ds(64 * q, 64)))
-            at = pl.ds(pl.multiple_of(128 * b + 64 * q, 64), 64)
+        pre = []
+        for line in range(8):
+            window = split3(get(xi, (), pl.ds(16 * line, 16)))
+            at = pl.ds(pl.multiple_of(128 * b + 16 * line, 16), 16)
             t_hi[at, :] = window[0]
             t_lo[at, :] = window[1]
-            firsts = []
-            for line in range(4):
-                at = slice(16 * line, 16 * line + 16)
-                firsts.append(dot(w_x[...], six([part[at] for part in window], ones)))
-            first = jnp.tanh(rows(*firsts))
-            f_hi, f_lo, s_hi, s_lo, gate_rows = upper_layers(first)
-            at = pl.ds(pl.multiple_of(256 * b + 128 * q, 128), 128)
-            h1_hi[at, :] = f_hi
-            h1_lo[at, :] = f_lo
-            h2_hi[at, :] = s_hi
-            h2_lo[at, :] = s_lo
-            put(gi, (), pl.ds(32 * q, 32), gate_rows)
-        gates = [get(gi, (), pl.ds(g, 8, stride=8)) for g in range(8)]
+            pre.append(dot(w_x[...], six(window, ones)))
+        yield
+        firsts, pre = middle(pre)
+        for line in range(8):
+            at = pl.ds(pl.multiple_of(256 * b + 32 * line, 32), 32)
+            h1_hi[at, :] = firsts[line][0]
+            h1_lo[at, :] = firsts[line][1]
+        yield
+        seconds, pre = output(pre)
+        for line in range(8):
+            at = pl.ds(pl.multiple_of(256 * b + 32 * line, 32), 32)
+            h2_hi[at, :] = seconds[line][0]
+            h2_lo[at, :] = seconds[line][1]
+        yield
+        gates = natural_gates(pre, gi)
         for g in range(8):
             gate_x[g, pl.ds(n0, 8), :] = gates[g]
         _, _, left, right = face_states(cells, gates)
@@ -317,26 +330,25 @@
         at = pl.ds(pl.multiple_of(32 * b, 32), 32)
         for ref, part in zip((mid_hi, mid_lo, mid_lo2), split3(get(mi, (), pl.ds(0, 32)))):
             ref[at, :] = part
-        return carry
-
-    lax.fori_loop(0, blocks + 1, x_forward, 0)
-    mid[:, :, 8 + own : 16 + own, :] = mid[:, :, 0:8, :]
-    for ref in (mid_hi, mid_lo, mid_lo2):
-        ref[4 * own + 32 : 4 * own + 64, :] = ref[0:32, :]
+        yield
+
     d_mix[:, 0:16, :] = jnp.zeros((2, 16, 128), F32)
 
-    def y_sweep(b, carry):
+    def y_sweep(b, valid):
         n0 = pl.multiple_of(8 * b, 8)
-        saved, windows = [], []
+        windows, pre = [], []
         for q in range(2):
             at = pl.ds(pl.multiple_of(32 * b + 16 * q, 16), 32)
             window = mid_hi[at, :], mid_lo[at, :], mid_lo2[at, :]
             windows.append(rows(window[0], window[1], ones))
-            first = jnp.tanh(dot(w_y[...], six(window, ones)))
-            parts = upper_layers(first)
-            saved.append(parts)
-            put(gi, (), pl.ds(32 * q, 32), parts[4])
-        gates = [get(gi, (), pl.ds(g, 8, stride=8)) for g in range(8)]
+            four = dot(w_y[...], six(window, ones))
+            pre += [four[32 * line : 32 * line + 32] for line in range(4)]
+        yield
+        firsts, pre = middle(pre)
+        yield
+        seconds, pre = output(pre)
+        yield
+        gates = natural_gates(pre, gi_y)
         cells = [[get(mid, (c,), pl.ds(n0 + k, 8)) for c in Y_ORDER] for k in range(4)]
         cots = [courant * (get(cot, (c,), pl.ds(n0 + 2, 8)) - get(cot, (c,), pl.ds(n0 + 1, 8))) for c in Y_ORDER]
         d_gates, minus_below, to_here, to_above, minus_above2 = flux_back(cells, gates, cots)
@@ -347,36 +359,31 @@
             put(face, (8 + to,), pl.ds(n0, 8), to_above[c])
             put(face, (12 + to,), pl.ds(n0, 8), minus_above2[c])
 
-        def load(part):
-            def of(pair):
-                at = slice(64 * (pair % 2), 64 * (pair % 2) + 64)
-                return saved[pair // 2][part][at], saved[pair // 2][part + 1][at]
-            return of
-
-        d_first = limiter_back(gates, d_gates, load(0), load(2))
-        outs, right_side = [], []
+        def load(parts):
+            return lambda pair: [rows(parts[2 * pair][k], parts[2 * pair + 1][k]) for k in range(2)]
+
+        outs, pres = back_output(gates, d_gates, di_y, load(seconds))
+        yield
+        d_second, pres = back_through(pres, load(seconds), w_mt)
+        yield
+        d_first, _ = back_through(pres, load(firsts), None)
+        combined, right_side = [], []
         for q in range(2):
             hi = rows(d_first[2 * q][0], d_first[2 * q + 1][0])
             lo = rows(d_first[2 * q][1], d_first[2 * q + 1][1])
-            outs.append(dot(w_yt[...], rows(hi, lo, hi)))
+            combined.append(dot(w_yt[...], rows(hi, lo, hi)))
             right_side.append(rows(hi, lo))
+        yield
+        weight_sums(outs, d_second, load(firsts), load(seconds), acc_my, acc_oy, valid)
+        yield
+        acc_y[...] += jnp.where(valid, dot_nt(lanes(*windows), lanes(*right_side)), 0.0)
         at = pl.multiple_of(32 * b, 32)
-        put(d_mix, (), pl.ds(at, 16), get(d_mix, (), pl.ds(at, 16)) + outs[0][:16])
-        put(d_mix, (), pl.ds(at + 16, 16), outs[0][16:] + outs[1][:16])
-        put(d_mix, (), pl.ds(at + 32, 16), outs[1][16:])
-        acc_y[...] += dot_nt(lanes(*windows), lanes(*right_side))
-
-        @pl.when(b == 0)
-        def _():
-            acc_y[...] = jnp.zeros_like(acc_y)
-            acc_m[...] = jnp.zeros_like(acc_m)
-            acc_o[...] = jnp.zeros_like(acc_o)
-
-        return carry
-
-    lax.fori_loop(0, blocks + 1, y_sweep, 0)
-
-    def x_back(b, carry):
+        put(d_mix, (), pl.ds(at, 16), get(d_mix, (), pl.ds(at, 16)) + combined[0][:16])
+        put(d_mix, (), pl.ds(at + 16, 16), combined[0][16:] + combined[1][:16])
+        put(d_mix, (), pl.ds(at + 32, 16), combined[1][16:])
+        yield
+
+    def x_back(b, valid):
         n0 = pl.multiple_of(8 * b, 8)
         gates = [gate_x[g, pl.ds(n0, 8), :] for g in range(8)]
         here = [nat[c, pl.ds(n0, 8), :] for c in range(4)]
@@ -396,7 +403,15 @@
                 return hi_ref[at, :], lo_ref[at, :]
             return of
 
-        d_first = limiter_back(gates, d_gates, load(h1_hi, h1_lo), load(h2_hi, h2_lo))
+        first, second = load(h1_hi, h1_lo), load(h2_hi, h2_lo)
+        outs, pres = back_output(gates, d_gates, di, second)
+        direct = [
+            (back[c] + to_here[c], minus_below[c], to_above[c], minus_above2[c]) for c in range(4)
+        ]
+        yield
+        d_second, pres = back_through(pres, second, w_mt)
+        yield
+        d_first, _ = back_through(pres, first, None)
         left_side, right_side = [], []
         for line in range(8):
             at = pl.ds(pl.multiple_of(128 * b + 16 * line, 16), 16)
@@ -405,21 +420,34 @@
             hi, lo = [v[at] for v in d_first[line // 2]]
             right_side.append(rows(hi, lo))
             put(zi, (), pl.ds(16 * line, 16), dot(w_xt[...], rows(hi, lo, hi)))
-        acc_x[...] += dot_nt(lanes(*left_side), lanes(*right_side))
+        yield
+        weight_sums(outs, d_second, first, second, acc_m, acc_o, valid)
+        acc_x[...] += jnp.where(valid, dot_nt(lanes(*left_side), lanes(*right_side)), 0.0)
+        yield
         for c in range(4):
             parts = [get(zi, (), pl.ds(4 * s + c, 8, stride=16)) for s in range(4)]
-            value = back[c] + to_here[c] + parts[1] + roll(parts[0] - minus_below[c], -1)
-            value = value + roll(to_above[c] + parts[2], 1) + roll(parts[3] - minus_above2[c], 2)
+            value = direct[c][0] + parts[1] + roll(parts[0] - direct[c][1], -1)
+            value = value + roll(direct[c][2] + parts[2], 1) + roll(parts[3] - direct[c][3], 2)
             out_nat[c, pl.ds(pl.multiple_of(n0 - 8, 8), 8), :] = value
+        yield
+
+    def step(i, carry):
+        back = x_back(jnp.maximum(i - 3, 1), i >= 4)
+        sweep = y_sweep(jnp.maximum(i - 2, 0), jnp.logical_and(i >= 3, i <= blocks + 2))
+        ahead = x_forward(i)
+        for stage in STAGES:
+            next({"b": back, "y": sweep, "f": ahead}[stage])
         return carry
 
-    lax.fori_loop(1, blocks + 1, x_back, 0)
+    lax.fori_loop(0, blocks + 4, step, 0)
 
     g_density[0] = out_nat[0].T
     g_momentum[0, 0] = out_nat[1].T
     g_momentum[0, 1] = out_nat[2].T
     g_tracer[0] = out_nat[3].T
 
+    acc_m[...] += acc_my[...]
+    acc_o[...] += acc_oy[...]
     r, k = index((24, 48), 0), index((24, 48), 1)
     pick = jnp.where(k < 32, k % 16, jnp.where(k == 32, 16, -1))
     first_x = exact(indicator(r == pick), acc_x[...])
@@ -528,8 +556,8 @@
         halo = jnp.concatenate([from_right, from_left], 1)
         biases = [b.reshape(1, -1) for b in (b_in, b_mid, b_out)]
         weights = (w_in, biases[0], w_mid, biases[1], w_out, biases[2])
-        extra = own + 16
-        lines = own + 8
+        extra = own + 32
+        lines = own + 32
         out = pl.pallas_call(
             kernel,
             out_shape=(
@@ -560,10 +588,14 @@
                 pltpu.VMEM((2, 128, 128), F32),
                 pltpu.VMEM((2, 64, 128), F32),
                 pltpu.VMEM((2, 64, 128), F32),
+                pltpu.VMEM((2, 64, 128), F32),
+                pltpu.VMEM((2, 64, 128), F32),
                 pltpu.VMEM((2, 32, 128), F32),
                 pltpu.VMEM((2, 128, 128), F32),
                 pltpu.VMEM((48, 64), F32),
                 pltpu.VMEM((80, 256), F32),
+                pltpu.VMEM((64, 80), F32),
+                pltpu.VMEM((32, 144), F32),
                 pltpu.VMEM((64, 80), F32),
                 pltpu.VMEM((32, 144), F32),
                 pltpu.VMEM((32, 112), BF16),

time: 109 us -> 81.9 us (0.75)
  Pallas kernels: 83 us -> 56.1 us
    pallas_call x1, Pallas kernels: 67.3 us -> 40.4 us  [body(): pl.pallas_call(kernel, out_shape=(jax.ShapeDtypeStruct(density.shape, F32...]
where the time goes in v2:
time: 81.9 us; the launch traced here: 80.8 us
  Pallas kernels  56.1 us (68%)
  starting transfers between devices  9.05 us (11%)
  waiting for transfers between devices  8.95 us (11%)
  local copies, waits for them, and re-layouts  5.25 us (6%)
    pallas_call x1, Pallas kernels, body(): pl.pallas_call(kernel, out_shape=(jax.ShapeDtypeStruct(density.shape, F32...  40.4 us
    pallas_call x1, Pallas kernels, body(): pl.pallas_call(functools.partial(reduce_kernel, sizes), out_shape=jax.Sha...  14.3 us
    ppermute x1, starting transfers between devices, body(): lax.ppermute(low, RING, [((i + 1) % size, i) for i in range(size)])  9.04 us
    ppermute x1, waiting for transfers between devices, body(): lax.ppermute(high, RING, [(i, (i + 1) % size) for i in range(size)])  8.04 us
    unnamed x14, local copies, waits for them, and re-layouts  5.24 us
  transfers between devices with their start and end apart: 2, of which 2 were waited for; matrix products, arithmetic and copies ran while one was open for 1% of the time, Pallas kernels for 0%

profile of v2, /device:TPU:0, one launch (start us, length us, event | category | flops | bytes accessed | tf_op | source)
XLA Modules:
  0.0 80.8 jit_solution(17934674845347653506)
XLA Ops:
  0.6 0.0 copy-start
  0.7 1.3 %copy.22 = f32[1,4,256,128]{2,3,1,0:T(8,128)S(1)} copy(f32[1,4,256,128]{3,2,1,0:T(8,128)} %cotangent.1) | data formatting | bytes 1048576 | tf_op args[3]
  1.9 0.0 copy-done
  2.0 0.0 copy-start.1
  2.0 0.1 copy.21
  2.1 0.8 copy-done.1
  2.9 0.0 copy-start.2
  2.9 0.1 copy.19
  3.0 0.8 copy-done.2
  3.8 0.1 copy.20
  3.9 0.1 maximum_bitcast_fusion
  3.9 0.0 copy-start.3
  4.0 9.0 %collective-permute-start = (f32[8,4,256]{2,1,0:T(4,128)S(1)}, f32[8,4,256]{2,1,0:T(4,128)S(1)}, u32[]{:S(2)}, u32[]{:S(2)}) collective-permute-start(f32[8,4,256]{2,1,0:T(4,128)S(1)} %get-tuple-element.38), channel_id=1, source_target_pairs={{1,0},{2,1},{3,2},{4,3},{5,4},{6,5},{7,6},{8,7},{9,8},{10,9},{11,1... | collective-permute-start | bytes 98312 | tf_op jit(solution)/shard_map/ppermute | solution.py:554
  13.0 0.0 collective-permute-start.1
  13.0 0.0 copy-done.3
  13.0 0.7 copy.23.w_in
  13.7 0.9 %collective-permute-done = f32[8,4,256]{2,1,0:T(4,128)S(1)} collective-permute-done((f32[8,4,256]{2,1,0:T(4,128)S(1)}, f32[8,4,256]{2,1,0:T(4,128)S(1)}, u32[]{:S(2)}, u32[]{:S(2)}) %collective-permute-start) | collective-permute-done | bytes 32800 | tf_op jit(solution)/shard_map/ppermute | solution.py:554
  14.6 8.0 %collective-permute-done.1 = f32[8,4,256]{2,1,0:T(4,128)S(1)} collective-permute-done((f32[8,4,256]{2,1,0:T(4,128)S(1)}, f32[8,4,256]{2,1,0:T(4,128)S(1)}, u32[]{:S(2)}, u32[]{:S(2)}) %collective-permute-start.1) | collective-permute-done | bytes 32800 | tf_op jit(solution)/shard_map/ppermute | solution.py:555
  22.7 0.6 pad_maximum_fusion.halo
  23.3 40.4 %shard_map.169 = (f32[1,256,128]{2,1,0:T(8,128)}, f32[1,2,256,128]{3,2,1,0:T(8,128)}, f32[1,256,128]{2,1,0:T(8,128)}, f32[48,128]{1,0:T(8,128)}) custom-call(f32[1,256,128]{2,1,0:T(8,128)} %density.1, f32[1,2,256,128]{3,2,1,0:T(8,128)} %momentum.1, f32[1,256,128]{2,1,0:T(8,128)} %tracer.1, f32[1,4,256,128]{3,2,1,0:T(8,128)} %cotangent.1, ...), custom_call_target="tpu_custom_call" | custom-call | tf_op jit(solution)/shard_map/pallas_call | solution.py:561
  63.8 14.3 %shard_map.170.total = f32[48,128]{1,0:T(8,128)} custom-call(f32[48,128]{1,0:T(8,128)} %get-tuple-element.22.mine), custom_call_target="tpu_custom_call" | custom-call | tf_op jit(solution)/shard_map/pallas_call | solution.py:614
  78.0 1.4 %shard_map.171 = (f32[32,16]{1,0:T(8,128)}, f32[1,32]{1,0:T(1,128)}, f32[32,32]{1,0:T(8,128)}, f32[1,32]{1,0:T(1,128)}, f32[8,32]{1,0:T(8,128)}, /*index=5*/f32[1,8]{1,0:T(1,128)}) custom-call(f32[48,128]{1,0:T(8,128)} %shard_map.170.total), custom_call_target="tpu_custom_call" | custom-call | tf_op jit(solution)/shard_map/pallas_call | solution.py:623
  79.4 1.4 %copy.24 = f32[32,16]{0,1:T(8,128)} copy(f32[32,16]{1,0:T(8,128)} %get-tuple-element.32) | data formatting | bytes 4096
  (1 shorter events, 0.0 us)
Async XLA Ops:
  0.6 1.3 %copy-start = (f32[1,2,256,128]{3,2,1,0:T(8,128)S(1)}, f32[1,2,256,128]{3,2,1,0:T(8,128)}, u32[]{:S(2)}) copy-start(f32[1,2,256,128]{3,2,1,0:T(8,128)} %momentum.1) | copy-start | bytes 786436
  2.0 0.9 %copy-start.1 = (f32[1,256,128]{2,1,0:T(8,128)S(1)}, f32[1,256,128]{2,1,0:T(8,128)}, u32[]{:S(2)}) copy-start(f32[1,256,128]{2,1,0:T(8,128)} %density.1) | copy-start | bytes 393220
  2.9 0.9 %copy-start.2 = (f32[1,256,128]{2,1,0:T(8,128)S(1)}, f32[1,256,128]{2,1,0:T(8,128)}, u32[]{:S(2)}) copy-start(f32[1,256,128]{2,1,0:T(8,128)} %tracer.1) | copy-start | bytes 393220
  3.9 9.1 %copy-start.3 = (f32[32,16]{0,1:T(8,128)S(1)}, f32[32,16]{0,1:T(8,128)}, u32[]{:S(2)}) copy-start(f32[32,16]{0,1:T(8,128)} %param.14) | copy-start | bytes 6148
  4.0 10.6 %collective-permute-start = (f32[8,4,256]{2,1,0:T(4,128)S(1)}, f32[8,4,256]{2,1,0:T(4,128)S(1)}, u32[]{:S(2)}, u32[]{:S(2)}) collective-permute-start(f32[8,4,256]{2,1,0:T(4,128)S(1)} %get-tuple-element.38), channel_id=1, source_target_pairs={{1,0},{2,1},{3,2},{4,3},{5,4},{6,5},{7,6},{8,7},{9,8},{10,9},{11,1... | collective-permute-start | bytes 98312 | tf_op jit(solution)/shard_map/ppermute | solution.py:554
  13.0 9.6 %collective-permute-start.1 = (f32[8,4,256]{2,1,0:T(4,128)S(1)}, f32[8,4,256]{2,1,0:T(4,128)S(1)}, u32[]{:S(2)}, u32[]{:S(2)}) collective-permute-start(f32[8,4,256]{2,1,0:T(4,128)S(1)} %get-tuple-element.39), channel_id=1, source_target_pairs={{0,1},{1,2},{2,3},{3,4},{4,5},{5,6},{6,7},{7,8},{8,9},{9,10},{10,1... | collective-permute-start | bytes 98312 | tf_op jit(solution)/shard_map/ppermute | solution.py:555

commit v3 on v2

--- a/solution.py
+++ b/solution.py
@@ -12,7 +12,6 @@
 courant = 0.1
 slope_gain = 0.25
 HALO = 4
-RING = ("tx", "ty")
 Y_ORDER = (0, 2, 1, 3)
 STAGES = "bybybybyfbyfyfyfy"
 
@@ -232,11 +231,15 @@
         else:
             source = momentum[0, c - 1]
         nat[c, 8 : 8 + own, :] = source.T
-        nat[c, 0:8, :] = halo[c]
-        nat[c, 8 + own : 16 + own, :] = halo[c]
+        for side in range(2):
+            edge = halo[side, 4 * c : 4 * c + 4, :]
+            nat[c, 4 * side : 4 * side + 4, :] = edge
+            nat[c, 8 + own + 4 * side : 12 + own + 4 * side, :] = edge
         put(cot, (c,), pl.ds(8, own), cotangent[0, c].T)
-        put(cot, (c,), pl.ds(0, 8), halo[4 + c])
-        put(cot, (c,), pl.ds(8 + own, 8), halo[4 + c])
+        for side in range(2):
+            edge = halo[side, 16 + 4 * c : 20 + 4 * c, :]
+            put(cot, (c,), pl.ds(4 * side, 4), edge)
+            put(cot, (c,), pl.ds(8 + own + 4 * side, 4), edge)
     acc_x[...] = jnp.zeros_like(acc_x)
     acc_y[...] = jnp.zeros_like(acc_y)
     acc_m[...] = jnp.zeros_like(acc_m)
@@ -489,6 +492,48 @@
     packed[40:48, :] = jnp.where(
         r == 0, first_bias, jnp.where(r == 1, second_bias, jnp.where(r == 2, out_bias, 0.0))
     )
+
+
+def halo_kernel(size, inner, density, momentum, tracer, cotangent, halo, sent, landed, send_sem, recv_sem):
+    mesh_ids = pl.DeviceIdType.MESH
+    here = lax.axis_index("tx") * inner + lax.axis_index("ty")
+    peers = []
+    for step in (size - 1, 1):
+        peer = lax.rem(here + step, size)
+        peers.append({"tx": peer // inner, "ty": lax.rem(peer, inner)})
+    barrier = pltpu.get_barrier_semaphore()
+    for peer in peers:
+        pl.semaphore_signal(barrier, inc=1, device_id=peer, device_id_type=mesh_ids)
+    own = density.shape[2]
+    for c in range(8):
+        if c >= 4:
+            source = cotangent[0, c - 4]
+        elif c == 0:
+            source = density[0]
+        elif c == 3:
+            source = tracer[0]
+        else:
+            source = momentum[0, c - 1]
+        lines = source.T
+        sent[0, 4 * c : 4 * c + 4, :] = lines[:HALO]
+        sent[1, 4 * c : 4 * c + 4, :] = lines[own - HALO :]
+    pl.semaphore_wait(barrier, 2)
+    copies = [
+        pltpu.make_async_remote_copy(
+            src_ref=sent.at[side],
+            dst_ref=landed.at[side],
+            send_sem=send_sem.at[side],
+            recv_sem=recv_sem.at[side],
+            device_id=peers[side],
+            device_id_type=mesh_ids,
+        )
+        for side in range(2)
+    ]
+    for copy in copies:
+        copy.start()
+    for copy in copies:
+        copy.wait()
+    halo[...] = landed[...]
 
 
 GROUPS = ("traj", "ty", "tx")
@@ -545,15 +590,19 @@
     return mesh.shape["tx"] * mesh.shape["ty"]
 
 
-def make_body(size, sizes):
+def make_body(size, inner, sizes):
     def body(density, momentum, tracer, cotangent, w_in, b_in, w_mid, b_mid, w_out, b_out):
         own, width = density.shape[2], density.shape[1]
-        states = jnp.concatenate([density[:, None], momentum, tracer[:, None], cotangent], 1)[0]
-        low = jnp.swapaxes(states[:, :, :HALO], 1, 2)
-        high = jnp.swapaxes(states[:, :, own - HALO :], 1, 2)
-        from_right = lax.ppermute(low, RING, [((i + 1) % size, i) for i in range(size)])
-        from_left = lax.ppermute(high, RING, [(i, (i + 1) % size) for i in range(size)])
-        halo = jnp.concatenate([from_right, from_left], 1)
+        in_vmem = pl.BlockSpec(memory_space=pltpu.VMEM)
+        halo_shape = (2, 8 * HALO, width)
+        halo = pl.pallas_call(
+            functools.partial(halo_kernel, size, inner),
+            out_shape=jax.ShapeDtypeStruct(halo_shape, F32),
+            in_specs=[in_vmem] * 4,
+            out_specs=in_vmem,
+            scratch_shapes=[pltpu.VMEM(halo_shape, F32)] * 2 + [pltpu.SemaphoreType.DMA((2,))] * 2,
+            compiler_params=pltpu.CompilerParams(collective_id=1, has_side_effects=True),
+        )(density, momentum, tracer, cotangent)
         biases = [b.reshape(1, -1) for b in (b_in, b_mid, b_out)]
         weights = (w_in, biases[0], w_mid, biases[1], w_out, biases[2])
         extra = own + 32
@@ -609,7 +658,6 @@
             ],
             compiler_params=pltpu.CompilerParams(vmem_limit_bytes=60 * 1024 * 1024),
         )(density, momentum, tracer, cotangent, halo, *weights)
-        in_vmem = pl.BlockSpec(memory_space=pltpu.VMEM)
         shape = (48, 128)
         total = pl.pallas_call(
             functools.partial(reduce_kernel, sizes),
@@ -656,5 +704,5 @@
         P(), P(), P(), P(), P(), P(),
     )
     return jax.shard_map(
-        make_body(ring_size(mesh), tuple(mesh.shape[axis] for axis in GROUPS)), mesh=mesh, in_specs=in_specs, out_specs=out_specs, check_vma=False
+        make_body(ring_size(mesh), mesh.shape["ty"], tuple(mesh.shape[axis] for axis in GROUPS)), mesh=mesh, in_specs=in_specs, out_specs=out_specs, check_vma=False
     )

time: 81.9 us -> 77.3 us (0.944)
  Pallas kernels: 56.1 us -> 73.5 us
  starting transfers between devices: 9.05 us -> 0 us
  waiting for transfers between devices: 8.95 us -> 0 us
  local copies, waits for them, and re-layouts: 5.25 us -> 2.76 us
    pallas_call x0 -> x1, Pallas kernels: none -> 13.6 us  [body(): pl.pallas_call(functools.partial(halo_kernel, size, inner), out_shape=jax...]
    ppermute x2 -> x0, starting transfers between devices: 9.05 us -> none  [the longest x1 9.04 us: body(): lax.ppermute(low, RING, [((i + 1) % size, i) for i in range(size)])]
    ppermute x2 -> x0, waiting for transfers between devices: 8.95 us -> none  [the longest x1 8.04 us: body(): lax.ppermute(high, RING, [(i, (i + 1) % size) for i in range(size)])]
    pallas_call x1, Pallas kernels: 14.3 us -> 18 us  [body(): pl.pallas_call(functools.partial(reduce_kernel, sizes), out_shape=jax.Sha...]
    unnamed x14 -> x2, local copies, waits for them, and re-layouts: 5.24 us -> 2.76 us
  transfers between devices with their start and end apart: 2 -> 0, of which waited for: 2 -> 0; matrix products, arithmetic and copies ran while one was open for 1% -> 0% of each run, Pallas kernels for 0% -> 0%
where the time goes in v3:
time: 77.3 us; the launch traced here: 76.9 us
  Pallas kernels  73.5 us (95%)
  local copies, waits for them, and re-layouts  2.76 us (4%)
    pallas_call x1, Pallas kernels, body(): pl.pallas_call(kernel, out_shape=(jax.ShapeDtypeStruct(density.shape, F32...  40.5 us
    pallas_call x1, Pallas kernels, body(): pl.pallas_call(functools.partial(reduce_kernel, sizes), out_shape=jax.Sha...  18 us
    pallas_call x1, Pallas kernels, body(): pl.pallas_call(functools.partial(halo_kernel, size, inner), out_shape=jax...  13.6 us
    unnamed x2, local copies, waits for them, and re-layouts  2.76 us

profile of v3, /device:TPU:0, one launch (start us, length us, event | category | flops | bytes accessed | tf_op | source)
XLA Modules:
  0.0 76.9 jit_solution(8950044369958459723)
XLA Ops:
  0.6 1.4 %copy.19.w_in = f32[32,16]{1,0:T(8,128)} copy(f32[32,16]{0,1:T(8,128)} %param.14) | data formatting | bytes 4096 | tf_op args[4]
  2.0 13.6 %shard_map.169.halo = f32[2,32,256]{2,1,0:T(8,128)} custom-call(f32[1,256,128]{2,1,0:T(8,128)} %density.3, f32[1,2,256,128]{3,2,1,0:T(8,128)} %momentum.3, f32[1,256,128]{2,1,0:T(8,128)} %tracer.3, f32[1,4,256,128]{3,2,1,0:T(8,128)} %cotangent.3), custom_call_target="tpu_custom_call" | custom-call | tf_op jit(solution)/shard_map/pallas_call | solution.py:598
  15.6 40.5 %shard_map.170 = (f32[1,256,128]{2,1,0:T(8,128)}, f32[1,2,256,128]{3,2,1,0:T(8,128)}, f32[1,256,128]{2,1,0:T(8,128)}, f32[48,128]{1,0:T(8,128)}) custom-call(f32[1,256,128]{2,1,0:T(8,128)} %density.3, f32[1,2,256,128]{3,2,1,0:T(8,128)} %momentum.3, f32[1,256,128]{2,1,0:T(8,128)} %tracer.3, f32[1,4,256,128]{3,2,1,0:T(8,128)} %cotangent.3, ...), custom_call_target="tpu_custom_call" | custom-call | tf_op jit(solution)/shard_map/pallas_call | solution.py:610
  56.1 18.0 %shard_map.171.total = f32[48,128]{1,0:T(8,128)} custom-call(f32[48,128]{1,0:T(8,128)} %get-tuple-element.22.mine), custom_call_target="tpu_custom_call" | custom-call | tf_op jit(solution)/shard_map/pallas_call | solution.py:662
  74.1 1.4 %shard_map.172 = (f32[32,16]{1,0:T(8,128)}, f32[1,32]{1,0:T(1,128)}, f32[32,32]{1,0:T(8,128)}, f32[1,32]{1,0:T(1,128)}, f32[8,32]{1,0:T(8,128)}, /*index=5*/f32[1,8]{1,0:T(1,128)}) custom-call(f32[48,128]{1,0:T(8,128)} %shard_map.171.total), custom_call_target="tpu_custom_call" | custom-call | tf_op jit(solution)/shard_map/pallas_call | solution.py:671
  75.5 1.4 %copy.20 = f32[32,16]{0,1:T(8,128)} copy(f32[32,16]{1,0:T(8,128)} %get-tuple-element.32) | data formatting | bytes 4096

commit v4 on v3

--- a/solution.py
+++ b/solution.py
@@ -144,7 +144,8 @@
 
 
 def fill_weights(given, filled):
-    w_in, b_in, w_mid, b_mid, w_out, b_out = [ref[...] for ref in given]
+    w_in_t, b_in, w_mid, b_mid, w_out, b_out = [ref[...] for ref in given]
+    w_in = w_in_t.T
     w_x, w_y, w_m, w_o, w_ot, w_mt, w_xt, w_yt = filled
 
     def bias_columns(bias, count, depth):
@@ -170,10 +171,16 @@
 
     sixfold = ((0, 3), (3, 5), (5, 6))
     threefold = ((0, 2), (2, 3))
-    for ref, weight, bias in ((w_x, w_in, b_in), (w_m, w_mid, b_mid), (w_o, w_out, b_out)):
+    for ref, weight, bias in ((w_x, w_in, b_in), (w_m, w_mid, b_mid)):
         units, count = weight.shape
         value = spread(split3(weight), sixfold, count, 6 * count + 16)
         ref[...] = (value + bias_columns(bias, units, 6 * count)).astype(BF16)
+    out_parts = split3(w_out)
+    for at, part in enumerate(out_parts):
+        value = spread([part], ((0, 3 - at),), 32, 112)
+        if at == 0:
+            value = value + bias_columns(b_out, 8, 96)
+        w_o[8 * at : 8 * at + 8, :] = value
     in_parts = split3(w_in)
     in_bias = bias_columns(b_in, 32, 192)
     for face in range(4):
@@ -253,7 +260,12 @@
 
     def output(pre):
         seconds = [split3(jnp.tanh(v)) for v in pre]
-        return seconds, [dot(w_o[...], six(v, ones)) for v in seconds]
+        weight = w_o[...].astype(BF16)
+        nexts = []
+        for v in seconds:
+            three = dot(weight, rows(*v, ones))
+            nexts.append(three[0:8] + (three[8:16] + three[16:24]))
+        return seconds, nexts
 
     def natural_gates(pre, gi):
         for line in range(8):
@@ -478,18 +490,18 @@
     r, k = index((8, 32), 0), index((8, 32), 1)
     summed = exact(indicator(r == k % 8), masked)
     r, k = index((144, 128), 0), index((144, 128), 1)
-    packed[0:32, :] = total
-    packed[32:40, :] = exact(summed, indicator(jnp.logical_and(r % 32 == k, r < 128)))
+    packed[0:8, :] = total[0:8] + exact(summed, indicator(jnp.logical_and(r % 32 + 96 == k, r < 128)))
+    packed[16:32, :] = total[16:32]
     out_bias = exact(indicator(index((8, 144), 1) == 128), acc_o[...], nt=True)
     r, k = index((32, 128), 0), index((32, 128), 1)
-    out_bias = exact(out_bias, indicator(r % 8 == k))
+    out_bias = exact(out_bias, indicator(r % 8 + 96 == k))
     r, k = index((32, 128), 0), index((32, 128), 1)
-    wide = indicator(r == k)
+    wide = indicator(r + 96 == k)
     first_bias = exact(first_bias[16:24], wide)
     second_bias = exact(second_bias, wide)
     r = index((8, 128), 0)
     first_bias = jnp.broadcast_to(first_bias[0:1], (8, 128))
-    packed[40:48, :] = jnp.where(
+    packed[8:16, :] = total[8:16] + jnp.where(
         r == 0, first_bias, jnp.where(r == 1, second_bias, jnp.where(r == 2, out_bias, 0.0))
     )
 
@@ -578,12 +590,12 @@
 
 
 def unpack_kernel(total, g_w_in, g_b_in, g_w_mid, g_b_mid, g_w_out, g_b_out):
-    g_w_in[...] = total[0:32, 64:80]
-    g_b_in[...] = total[40:41, 0:32]
+    g_w_in[...] = total[0:32, :].T[64:80]
+    g_b_in[...] = total[8:9, 96:128]
     g_w_mid[...] = total[0:32, 0:32]
-    g_b_mid[...] = total[41:42, 0:32]
-    g_w_out[...] = total[32:40, 0:32]
-    g_b_out[...] = total[42:43, 0:8]
+    g_b_mid[...] = total[9:10, 96:128]
+    g_w_out[...] = total[0:8, 96:128]
+    g_b_out[...] = total[10:11, 96:104]
 
 
 def ring_size(mesh):
@@ -604,7 +616,7 @@
             compiler_params=pltpu.CompilerParams(collective_id=1, has_side_effects=True),
         )(density, momentum, tracer, cotangent)
         biases = [b.reshape(1, -1) for b in (b_in, b_mid, b_out)]
-        weights = (w_in, biases[0], w_mid, biases[1], w_out, biases[2])
+        weights = (w_in.T, biases[0], w_mid, biases[1], w_out, biases[2])
         extra = own + 32
         lines = own + 32
         out = pl.pallas_call(
@@ -613,7 +625,7 @@
                 jax.ShapeDtypeStruct(density.shape, F32),
                 jax.ShapeDtypeStruct(momentum.shape, F32),
                 jax.ShapeDtypeStruct(tracer.shape, F32),
-                jax.ShapeDtypeStruct((48, 128), F32),
+                jax.ShapeDtypeStruct((32, 128), F32),
             ),
             in_specs=[pl.BlockSpec(memory_space=pltpu.VMEM)] * 11,
             out_specs=tuple([pl.BlockSpec(memory_space=pltpu.VMEM)] * 4),
@@ -650,7 +662,7 @@
                 pltpu.VMEM((32, 112), BF16),
                 pltpu.VMEM((128, 208), BF16),
                 pltpu.VMEM((32, 208), BF16),
-                pltpu.VMEM((8, 208), BF16),
+                pltpu.VMEM((24, 112), F32),
                 pltpu.VMEM((64, 48), BF16),
                 pltpu.VMEM((64, 192), BF16),
                 pltpu.VMEM((16, 96), BF16),
@@ -658,7 +670,7 @@
             ],
             compiler_params=pltpu.CompilerParams(vmem_limit_bytes=60 * 1024 * 1024),
         )(density, momentum, tracer, cotangent, halo, *weights)
-        shape = (48, 128)
+        shape = (32, 128)
         total = pl.pallas_call(
             functools.partial(reduce_kernel, sizes),
             out_shape=jax.ShapeDtypeStruct(shape, F32),
@@ -678,7 +690,7 @@
             out[0],
             out[1],
             out[2],
-            totals[0],
+            totals[0].T,
             totals[1].reshape(-1),
             totals[2],
             totals[3].reshape(-1),

time: 77.3 us -> 72.4 us (0.937)
  local copies, waits for them, and re-layouts: 2.76 us -> 0 us
  Pallas kernels: 73.5 us -> 71.5 us
    unnamed x2 -> x0, local copies, waits for them, and re-layouts: 2.76 us -> none
    pallas_call x1, Pallas kernels: 40.5 us -> 38.7 us  [body(): pl.pallas_call(kernel, out_shape=(jax.ShapeDtypeStruct(density.shape, F32...]
where the time goes in v4:
time: 72.4 us; the launch traced here: 72.2 us
  Pallas kernels  71.5 us (99%)
    pallas_call x1, Pallas kernels, body(): pl.pallas_call(kernel, out_shape=(jax.ShapeDtypeStruct(density.shape, F32...  38.7 us
    pallas_call x1, Pallas kernels, body(): pl.pallas_call(functools.partial(reduce_kernel, sizes), out_shape=jax.Sha...  17.7 us
    pallas_call x1, Pallas kernels, body(): pl.pallas_call(functools.partial(halo_kernel, size, inner), out_shape=jax...  13.7 us

profile of v4, /device:TPU:0, one launch (start us, length us, event | category | flops | bytes accessed | tf_op | source)
XLA Modules:
  0.0 72.2 jit_solution(6969044440942471469)
XLA Ops:
  0.6 13.7 %shard_map.169.halo = f32[2,32,256]{2,1,0:T(8,128)} custom-call(f32[1,256,128]{2,1,0:T(8,128)} %density.3, f32[1,2,256,128]{3,2,1,0:T(8,128)} %momentum.3, f32[1,256,128]{2,1,0:T(8,128)} %tracer.3, f32[1,4,256,128]{3,2,1,0:T(8,128)} %cotangent.3), custom_call_target="tpu_custom_call" | custom-call | tf_op jit(solution)/shard_map/pallas_call | solution.py:610
  14.3 38.7 %shard_map.170 = (f32[1,256,128]{2,1,0:T(8,128)}, f32[1,2,256,128]{3,2,1,0:T(8,128)}, f32[1,256,128]{2,1,0:T(8,128)}, f32[32,128]{1,0:T(8,128)}) custom-call(f32[1,256,128]{2,1,0:T(8,128)} %density.3, f32[1,2,256,128]{3,2,1,0:T(8,128)} %momentum.3, f32[1,256,128]{2,1,0:T(8,128)} %tracer.3, f32[1,4,256,128]{3,2,1,0:T(8,128)} %cotangent.3, ...), custom_call_target="tpu_custom_call" | custom-call | tf_op jit(solution)/shard_map/pallas_call | solution.py:622
  53.0 17.7 %shard_map.171.total = f32[32,128]{1,0:T(8,128)} custom-call(f32[32,128]{1,0:T(8,128)} %get-tuple-element.22.mine), custom_call_target="tpu_custom_call" | custom-call | tf_op jit(solution)/shard_map/pallas_call | solution.py:674
  70.7 1.4 %shard_map.172 = (f32[16,32]{1,0:T(8,128)}, f32[1,32]{1,0:T(1,128)}, f32[32,32]{1,0:T(8,128)}, f32[1,32]{1,0:T(1,128)}, f32[8,32]{1,0:T(8,128)}, /*index=5*/f32[1,8]{1,0:T(1,128)}) custom-call(f32[32,128]{1,0:T(8,128)} %shard_map.171.total), custom_call_target="tpu_custom_call" | custom-call | tf_op jit(solution)/shard_map/pallas_call | solution.py:683

commit v5 on v4

--- a/solution.py
+++ b/solution.py
@@ -13,7 +13,7 @@
 slope_gain = 0.25
 HALO = 4
 Y_ORDER = (0, 2, 1, 3)
-STAGES = "bybybybyfbyfyfyfy"
+STAGES = "bfybfybfybyfbyyyy"
 
 
 def split(x):
@@ -171,10 +171,14 @@
 
     sixfold = ((0, 3), (3, 5), (5, 6))
     threefold = ((0, 2), (2, 3))
-    for ref, weight, bias in ((w_x, w_in, b_in), (w_m, w_mid, b_mid)):
+    for ref, weight, bias in ((w_x, w_in, b_in),):
         units, count = weight.shape
         value = spread(split3(weight), sixfold, count, 6 * count + 16)
         ref[...] = (value + bias_columns(bias, units, 6 * count)).astype(BF16)
+    mid_parts = split3(w_mid)
+    upper = spread(mid_parts[:1], ((0, 3),), 32, 144) + bias_columns(b_mid, 32, 128)
+    lower = spread(mid_parts[1:], ((0, 2), (3, 4)), 32, 144)
+    w_m[...] = rows(upper, lower).astype(BF16)
     out_parts = split3(w_out)
     for at, part in enumerate(out_parts):
         value = spread([part], ((0, 3 - at),), 32, 112)
@@ -256,7 +260,11 @@
 
     def middle(pre):
         firsts = [split3(jnp.tanh(v)) for v in pre]
-        return firsts, [dot(w_m[...], six(v, ones)) for v in firsts]
+        nexts = []
+        for v in firsts:
+            two = dot(w_m[...], rows(*v, v[0], ones))
+            nexts.append(two[0:32] + two[32:64])
+        return firsts, nexts
 
     def output(pre):
         seconds = [split3(jnp.tanh(v)) for v in pre]
@@ -661,7 +669,7 @@
                 pltpu.VMEM((32, 144), F32),
                 pltpu.VMEM((32, 112), BF16),
                 pltpu.VMEM((128, 208), BF16),
-                pltpu.VMEM((32, 208), BF16),
+                pltpu.VMEM((64, 144), BF16),
                 pltpu.VMEM((24, 112), F32),
                 pltpu.VMEM((64, 48), BF16),
                 pltpu.VMEM((64, 192), BF16),

time: 72.4 us -> 74.5 us (1.029)
  Pallas kernels: 71.5 us -> 73.5 us
    pallas_call x1, Pallas kernels: 38.7 us -> 40.7 us  [body(): pl.pallas_call(kernel, out_shape=(jax.ShapeDtypeStruct(density.shape, F32...]
where the time goes in v5:
time: 74.5 us; the launch traced here: 74.2 us
  Pallas kernels  73.5 us (99%)
    pallas_call x1, Pallas kernels, body(): pl.pallas_call(kernel, out_shape=(jax.ShapeDtypeStruct(density.shape, F32...  40.7 us
    pallas_call x1, Pallas kernels, body(): pl.pallas_call(functools.partial(reduce_kernel, sizes), out_shape=jax.Sha...  17.7 us
    pallas_call x1, Pallas kernels, body(): pl.pallas_call(functools.partial(halo_kernel, size, inner), out_shape=jax...  13.7 us

profile of v5, /device:TPU:0, one launch (start us, length us, event | category | flops | bytes accessed | tf_op | source)
XLA Modules:
  0.0 74.2 jit_solution(15323584547651257462)
XLA Ops:
  0.6 13.7 %shard_map.169.halo = f32[2,32,256]{2,1,0:T(8,128)} custom-call(f32[1,256,128]{2,1,0:T(8,128)} %density.3, f32[1,2,256,128]{3,2,1,0:T(8,128)} %momentum.3, f32[1,256,128]{2,1,0:T(8,128)} %tracer.3, f32[1,4,256,128]{3,2,1,0:T(8,128)} %cotangent.3), custom_call_target="tpu_custom_call" | custom-call | tf_op jit(solution)/shard_map/pallas_call | solution.py:618
  14.3 40.7 %shard_map.170 = (f32[1,256,128]{2,1,0:T(8,128)}, f32[1,2,256,128]{3,2,1,0:T(8,128)}, f32[1,256,128]{2,1,0:T(8,128)}, f32[32,128]{1,0:T(8,128)}) custom-call(f32[1,256,128]{2,1,0:T(8,128)} %density.3, f32[1,2,256,128]{3,2,1,0:T(8,128)} %momentum.3, f32[1,256,128]{2,1,0:T(8,128)} %tracer.3, f32[1,4,256,128]{3,2,1,0:T(8,128)} %cotangent.3, ...), custom_call_target="tpu_custom_call" | custom-call | tf_op jit(solution)/shard_map/pallas_call | solution.py:630
  55.0 17.7 %shard_map.171.total = f32[32,128]{1,0:T(8,128)} custom-call(f32[32,128]{1,0:T(8,128)} %get-tuple-element.22.mine), custom_call_target="tpu_custom_call" | custom-call | tf_op jit(solution)/shard_map/pallas_call | solution.py:682
  72.8 1.4 %shard_map.172 = (f32[16,32]{1,0:T(8,128)}, f32[1,32]{1,0:T(1,128)}, f32[32,32]{1,0:T(8,128)}, f32[1,32]{1,0:T(1,128)}, f32[8,32]{1,0:T(8,128)}, /*index=5*/f32[1,8]{1,0:T(1,128)}) custom-call(f32[32,128]{1,0:T(8,128)} %shard_map.171.total), custom_call_target="tpu_custom_call" | custom-call | tf_op jit(solution)/shard_map/pallas_call | solution.py:691
